TPU v7x, 128 devices: a whole 4x4x4 slice. The times are simulated.
128 devices in a mesh: inp: 8 (over x_lo, z), tm: 16 (over x_hi, y, core).
Axes of the slice: x: 4 (x_hi: 2, x_lo: 2; x = x_hi * 2 + x_lo), y: 4, z: 4, core: 2. Of those that a mesh axis runs over, the one named last changes fastest.
Arguments:
- samples: bfloat16 [512, 1024, 1024], P('inp', 'tm'), may hold values from -6 to 6
- eq_gain: float32 [512, 512], P(None, 'inp'), may hold values from 0.5 to 2
Outputs:
- visibilities: float32 [512, 2, 512, 512], P(('inp', 'tm'))
All inputs are finite; a program needn't handle non-finite values.
Results may differ from a plain program's by a relative error of at most 0.0033.
Values may be sent and summed in bfloat16 or wider, within the bound.
No kernel may reach another device: no remote copies, remote signals or barrier semaphores. Data moves between devices by JAX's collectives and lax.ppermute only.
A program may use at most 192 MiB of HBM per device.

v0:
```python
import functools
import math

import jax
import jax.numpy as jnp
import ml_dtypes
import numpy as np
from jax import lax
from jax.experimental import pallas as pl
from jax.experimental.pallas import tpu as pltpu
from jax.sharding import PartitionSpec as P

TAPS = 4
CHUNKS = 2
BLOCK = 16
SUB = 4


def passed_along(array, axis, by):
    devices = lax.axis_size(axis)
    pairs = [(i, i + by) for i in range(devices) if 0 <= i + by < devices]
    return lax.ppermute(array, axis, pairs)


def window_table(taps, nfft):
    position = np.arange(taps * nfft, dtype=np.float64) + 0.5
    shape_part = np.sinc(position / nfft - taps / 2.0)
    taper = 0.5 - 0.5 * np.cos(position * (2.0 * math.pi / (taps * nfft)))
    return (shape_part * taper).reshape(taps, nfft).astype(np.float32)


def fourier_tables(channels, nfft, groups):
    chan = np.arange(channels)
    phase = (chan[:, None] * np.arange(nfft)[None, :] % nfft) * (2.0 * math.pi / nfft)
    scale = 1.0 / math.sqrt(nfft)
    table = np.stack([np.cos(phase) * scale, -np.sin(phase) * scale])
    table = table.astype(np.float32).astype(ml_dtypes.bfloat16)
    each = channels // groups // CHUNKS
    table = table.reshape(2, groups, CHUNKS, each, nfft).transpose(2, 0, 1, 3, 4)
    return table.reshape(CHUNKS, 2 * groups * each, nfft)


def channelize_kernel(table_ref, gain_ref, rows_ref, out_ref, turned):
    inputs, frames, nfft = rows_ref.shape
    count = table_ref.shape[0] // 2
    table = table_ref[...]
    lane = lax.broadcasted_iota(jnp.int32, (count, 2 * frames), 1)
    first = lane < frames
    for s in range(inputs // SUB):
        rows = rows_ref[s * SUB : (s + 1) * SUB].reshape(SUB * frames, nfft)
        both = lax.dot_general(
            table, rows, (((1,), (1,)), ((), ())), preferred_element_type=jnp.float32
        )
        for j in range(SUB // 2):
            real = both[:count, j * 2 * frames : (j + 1) * 2 * frames]
            imag = both[count:, j * 2 * frames : (j + 1) * 2 * frames]
            even = jnp.where(first, real, pltpu.roll(imag, frames, 1))
            odd = jnp.where(first, pltpu.roll(real, frames, 1), imag)
            a = s * SUB + 2 * j
            turned[pl.ds(a, count, stride=inputs), :] = even * gain_ref[0, :, a : a + 1]
            turned[pl.ds(a + 1, count, stride=inputs), :] = odd * gain_ref[0, :, a + 1 : a + 2]
    out_ref[...] = turned[...].reshape(count, inputs, 2 * frames).astype(out_ref.dtype)


def channelize(table, gain, filtered):
    inputs, frames, nfft = filtered.shape
    count = table.shape[0] // 2
    return pl.pallas_call(
        channelize_kernel,
        grid=(inputs // BLOCK,),
        in_specs=[
            pl.BlockSpec(table.shape, lambda i: (0, 0)),
            pl.BlockSpec((1, count, BLOCK), lambda i: (i, 0, 0)),
            pl.BlockSpec((BLOCK, frames, nfft), lambda i: (i, 0, 0)),
        ],
        out_specs=pl.BlockSpec((count, BLOCK, 2 * frames), lambda i: (0, i, 0)),
        out_shape=jax.ShapeDtypeStruct((count, inputs, 2 * frames), jnp.bfloat16),
        scratch_shapes=[pltpu.VMEM((count * BLOCK, 2 * frames), jnp.float32)],
        compiler_params=pltpu.CompilerParams(
            dimension_semantics=("arbitrary",), vmem_limit_bytes=40 * 2**20
        ),
        cost_estimate=pl.CostEstimate(
            flops=4 * count * inputs * frames * nfft,
            transcendentals=0,
            bytes_accessed=2 * (inputs * frames * nfft + count * inputs * 2 * frames),
        ),
        name="channelize",
    )(table, gain, filtered)


def correlate_kernel(frames_all, blocks_ref, *refs):
    out_ref = refs[-1]
    n_time = blocks_ref.shape[1]
    inputs_all = blocks_ref.shape[0] * blocks_ref.shape[3]
    width = blocks_ref.shape[4]
    half = width // 2
    straight, crossed = [], []
    for t in range(n_time):
        part = blocks_ref[:, t, 0].reshape(inputs_all, width)
        straight.append(part)
        crossed.append(jnp.concatenate([part[:, half:], -part[:, :half]], axis=1))
    straight = jnp.concatenate(straight, axis=1)
    crossed = jnp.concatenate(crossed, axis=1)
    last = (((1,), (1,)), ((), ()))
    scale = 1.0 / frames_all
    out_ref[0, 0] = (
        lax.dot_general(straight, straight, last, preferred_element_type=jnp.float32) * scale
    )
    out_ref[0, 1] = (
        lax.dot_general(crossed, straight, last, preferred_element_type=jnp.float32) * scale
    )


def correlate(arrived, before, chunk, chan_dev, frames_all):
    n_inp, n_time, each, local, width = arrived.shape
    inputs_all = n_inp * local
    operands = [arrived]
    in_specs = [pl.BlockSpec((n_inp, n_time, 1, local, width), lambda i: (0, 0, i, 0, 0))]
    aliases = {}
    if before is not None:
        operands.append(before)
        in_specs.append(pl.BlockSpec(memory_space=pl.ANY))
        aliases = {1: 0}
    return pl.pallas_call(
        functools.partial(correlate_kernel, frames_all),
        grid=(each,),
        in_specs=in_specs,
        out_specs=pl.BlockSpec(
            (1, 2, inputs_all, inputs_all), lambda i: (chunk * each + i, 0, 0, 0)
        ),
        out_shape=jax.ShapeDtypeStruct((chan_dev, 2, inputs_all, inputs_all), jnp.float32),
        input_output_aliases=aliases,
        compiler_params=pltpu.CompilerParams(
            dimension_semantics=("arbitrary",), vmem_limit_bytes=40 * 2**20
        ),
        cost_estimate=pl.CostEstimate(
            flops=each * 4 * inputs_all * inputs_all * n_time * width,
            transcendentals=0,
            bytes_accessed=each * (2 * inputs_all * n_time * width + 8 * inputs_all * inputs_all),
        ),
        name="correlate",
    )(*operands)


def on_device(samples, eq_gain):
    local_inputs, local_frames, nfft = samples.shape
    channels = nfft // 2
    n_inp = lax.axis_size("inp")
    n_time = lax.axis_size("tm")
    groups = n_inp * n_time
    chan_dev = channels // groups
    each = chan_dev // CHUNKS
    frames_all = n_time * local_frames
    tail = samples[:, local_frames - (TAPS - 1) :, :]
    before = passed_along(tail, "tm", 1)
    padded = jnp.concatenate([before, samples], axis=1)
    window = window_table(TAPS, nfft)
    filtered = jnp.zeros((local_inputs, local_frames, nfft), jnp.float32)
    for tap in range(TAPS):
        filtered = filtered + window[tap] * padded[:, tap : tap + local_frames, :].astype(
            jnp.float32
        )
    filtered = filtered.astype(jnp.bfloat16)
    tables = fourier_tables(channels, nfft, groups)
    gains = eq_gain.reshape(groups, CHUNKS, each, local_inputs // BLOCK, BLOCK)
    gains = gains.transpose(1, 3, 0, 2, 4).reshape(
        CHUNKS, local_inputs // BLOCK, groups * each, BLOCK
    )
    visibilities = None
    for k in range(CHUNKS):
        parcel = channelize(jnp.asarray(tables[k]), gains[k], filtered)
        parcel = parcel.reshape(groups, each * local_inputs, 2 * local_frames)
        arrived = lax.all_to_all(
            parcel, ("inp", "tm"), split_axis=0, concat_axis=0, tiled=True
        )
        arrived = arrived.reshape(n_inp, n_time, each, local_inputs, 2 * local_frames)
        visibilities = correlate(arrived, visibilities, k, chan_dev, frames_all)
    return visibilities


def solution(mesh):
    placed = (P("inp", "tm", None), P(None, "inp"))
    return jax.shard_map(
        on_device,
        mesh=mesh,
        in_specs=placed,
        out_specs=P(("inp", "tm"), None, None, None),
        check_vma=False,
    )
```

profile of v0, /device:TPU:6, one launch (start us, length us, event | category | flops | bytes accessed | tf_op | source)
XLA Modules:
  0.0 176.3 jit_solution(9495880070677940510)
XLA Ops:
  0.0 1.5 slice.21
  1.5 1.9 %collective-permute-start = (bf16[64,3,1024]{2,1,0:T(4,128)(2,1)S(1)}, bf16[64,3,1024]{2,1,0:T(4,128)(2,1)S(1)}, u32[]{:S(2)}, u32[]{:S(2)}) collective-permute-start(bf16[64,3,1024]{2,1,0:T(4,128)(2,1)S(1)} %slice.21), channel_id=1, source_target_pairs={{0,1},{1,2},{2,3},{3,4},{4,5},{5,6},{6,7},{7,8},{8,9},{9,10},{10,1... | collective-permute-start | bytes 1179656 | tf_op jit(solution)/shard_map/ppermute | solution.py:22
  3.4 1.0 copy.11
  4.5 0.4 reshape.24
  4.9 0.2 fusion.2
  5.1 0.3 copy.13
  5.4 0.0 copy-start.5
  5.4 10.2 %collective-permute-done = bf16[64,3,1024]{2,1,0:T(4,128)(2,1)S(1)} collective-permute-done((bf16[64,3,1024]{2,1,0:T(4,128)(2,1)S(1)}, bf16[64,3,1024]{2,1,0:T(4,128)(2,1)S(1)}, u32[]{:S(2)}, u32[]{:S(2)}) %collective-permute-start) | collective-permute-done | bytes 393248 | tf_op jit(solution)/shard_map/ppermute | solution.py:22
  15.6 18.2 %add_convert_fusion.rows_ref = bf16[64,64,1024]{2,1,0:T(8,128)(2,1)S(1)} fusion(bf16[64,64,1024]{2,1,0:T(8,128)(2,1)} %param.8, bf16[64,3,1024]{2,1,0:T(4,128)(2,1)S(1)} %collective-permute-done, f32[1024]{0:T(1024)} %constant.15.clone, f32[1024]{0:T(1024)} %constant.14.clone, f32[1024]{0:T(1024)} %constant.13.clone, f32[1024]{0:T(1024)} %constant.12.clone), kind=kLoop, calls=%fused_computation | loop fusion | flops 88080384 | bytes 17186816 | tf_op jit(solution)/shard_map/convert_element_type | solution.py:163
  33.8 0.0 copy-done.5
  33.9 8.2 %channelize.3 = bf16[256,64,128]{2,1,0:T(8,128)(2,1)S(1)} custom-call(bf16[512,1024]{1,0:T(8,128)(2,1)S(1)} %copy-done.5, f32[4,256,16]{2,1,0:T(8,128)S(1)} %bitcast.9, bf16[64,64,1024]{2,1,0:T(8,128)(2,1)S(1)} %add_convert_fusion.rows_ref), custom_call_target="tpu_custom_call" | custom-call | flops 4294967296 | bytes 12582912 | tf_op jit(solution)/shard_map/channelize/pallas_call | solution.py:68
  42.1 0.0 copy-start
  42.1 3.4 %copy-done = bf16[64,64,1024]{2,1,0:T(8,128)(2,1)} copy-done((bf16[64,64,1024]{2,1,0:T(8,128)(2,1)}, bf16[64,64,1024]{2,1,0:T(8,128)(2,1)S(1)}, u32[]{:S(2)}) %copy-start) | copy-done | bytes 8388632
  45.5 0.0 copy-start.3
  45.5 2.0 %copy-done.3 = bf16[256,64,128]{2,1,0:T(8,128)(2,1)} copy-done((bf16[256,64,128]{2,1,0:T(8,128)(2,1)}, bf16[256,64,128]{2,1,0:T(8,128)(2,1)S(1)}, u32[]{:S(2)}) %copy-start.3) | copy-done | bytes 4194328
  47.4 0.0 copy-start.4
  47.4 8.3 %all-to-all-start.1 = ((bf16[128,128,128]{2,1,0:T(8,128)(2,1)}), bf16[128,128,128]{2,1,0:T(8,128)(2,1)}, u32[]{:S(2)}, u32[]{:S(2)}) async-start(bf16[128,128,128]{2,1,0:T(8,128)(2,1)} %bitcast.8), calls=%async_computation.1 | async-start | bytes 8388608 | tf_op jit(solution)/shard_map/all_to_all | solution.py:173
  55.7 0.3 copy.12
  56.0 0.0 copy-done.4
  56.0 0.0 copy-start.1
  56.0 3.4 %copy-done.1 = bf16[64,64,1024]{2,1,0:T(8,128)(2,1)S(1)} copy-done((bf16[64,64,1024]{2,1,0:T(8,128)(2,1)S(1)}, bf16[64,64,1024]{2,1,0:T(8,128)(2,1)}, u32[]{:S(2)}) %copy-start.1) | copy-done | bytes 8388632
  59.4 8.2 %channelize.2 = bf16[256,64,128]{2,1,0:T(8,128)(2,1)S(1)} custom-call(bf16[512,1024]{1,0:T(8,128)(2,1)S(1)} %copy-done.4, f32[4,256,16]{2,1,0:T(8,128)S(1)} %bitcast.10, bf16[64,64,1024]{2,1,0:T(8,128)(2,1)S(1)} %copy-done.1), custom_call_target="tpu_custom_call" | custom-call | flops 4294967296 | bytes 12582912 | tf_op jit(solution)/shard_map/channelize/pallas_call | solution.py:68
  67.6 0.0 copy-start.2
  67.6 2.0 %copy-done.2 = bf16[256,64,128]{2,1,0:T(8,128)(2,1)} copy-done((bf16[256,64,128]{2,1,0:T(8,128)(2,1)}, bf16[256,64,128]{2,1,0:T(8,128)(2,1)S(1)}, u32[]{:S(2)}) %copy-start.2) | copy-done | bytes 4194328
  69.6 38.8 %all-to-all-done.1 = bf16[128,128,128]{2,1,0:T(8,128)(2,1)} async-done(((bf16[128,128,128]{2,1,0:T(8,128)(2,1)}), bf16[128,128,128]{2,1,0:T(8,128)(2,1)}, u32[]{:S(2)}, u32[]{:S(2)}) %all-to-all-start.1) | async-done | bytes 4194336 | tf_op jit(solution)/shard_map/all_to_all | solution.py:173
  108.4 7.6 %all-to-all-start = ((bf16[128,128,128]{2,1,0:T(8,128)(2,1)}), bf16[128,128,128]{2,1,0:T(8,128)(2,1)}, u32[]{:S(2)}, u32[]{:S(2)}) async-start(bf16[128,128,128]{2,1,0:T(8,128)(2,1)} %bitcast.7), calls=%async_computation | async-start | bytes 8388608 | tf_op jit(solution)/shard_map/all_to_all | solution.py:173
  116.0 7.7 %correlate.2.refs_0_ = f32[4,2,512,512]{3,2,1,0:T(8,128)} custom-call(bf16[8,16,2,64,128]{4,3,2,1,0:T(8,128)(2,1)} %bitcast.6.blocks_ref), custom_call_target="tpu_custom_call" | custom-call | flops 4294967296 | bytes 8388608 | tf_op jit(solution)/shard_map/correlate/pallas_call | solution.py:124
  123.7 44.9 %all-to-all-done = bf16[128,128,128]{2,1,0:T(8,128)(2,1)} async-done(((bf16[128,128,128]{2,1,0:T(8,128)(2,1)}), bf16[128,128,128]{2,1,0:T(8,128)(2,1)}, u32[]{:S(2)}, u32[]{:S(2)}) %all-to-all-start) | async-done | bytes 4194336 | tf_op jit(solution)/shard_map/all_to_all | solution.py:173
  168.6 7.7 %correlate.3 = f32[4,2,512,512]{3,2,1,0:T(8,128)} custom-call(bf16[8,16,2,64,128]{4,3,2,1,0:T(8,128)(2,1)} %bitcast.3.blocks_ref, f32[4,2,512,512]{3,2,1,0:T(8,128)} %correlate.2.refs_0_), custom_call_target="tpu_custom_call", output_to_operand_aliasing={{}: (1, {})} | custom-call | flops 4294967296 | bytes 8388608 | tf_op jit(solution)/shard_map/correlate/pallas_call | solution.py:124
Async XLA Ops:
  1.5 14.1 %collective-permute-start = (bf16[64,3,1024]{2,1,0:T(4,128)(2,1)S(1)}, bf16[64,3,1024]{2,1,0:T(4,128)(2,1)S(1)}, u32[]{:S(2)}, u32[]{:S(2)}) collective-permute-start(bf16[64,3,1024]{2,1,0:T(4,128)(2,1)S(1)} %slice.21), channel_id=1, source_target_pairs={{0,1},{1,2},{2,3},{3,4},{4,5},{5,6},{6,7},{7,8},{8,9},{9,10},{10,1... | collective-permute-start | bytes 1179656 | tf_op jit(solution)/shard_map/ppermute | solution.py:22
  5.4 28.5 %copy-start.5 = (bf16[512,1024]{1,0:T(8,128)(2,1)S(1)}, bf16[512,1024]{1,0:T(8,128)(2,1)}, u32[]{:S(2)}) copy-start(bf16[512,1024]{1,0:T(8,128)(2,1)} %constant.16.clone.table_ref) | copy-start | bytes 3145732
  42.1 3.4 %copy-start = (bf16[64,64,1024]{2,1,0:T(8,128)(2,1)}, bf16[64,64,1024]{2,1,0:T(8,128)(2,1)S(1)}, u32[]{:S(2)}) copy-start(bf16[64,64,1024]{2,1,0:T(8,128)(2,1)S(1)} %add_convert_fusion.rows_ref) | copy-start | bytes 25165828
  45.5 2.0 %copy-start.3 = (bf16[256,64,128]{2,1,0:T(8,128)(2,1)}, bf16[256,64,128]{2,1,0:T(8,128)(2,1)S(1)}, u32[]{:S(2)}) copy-start(bf16[256,64,128]{2,1,0:T(8,128)(2,1)S(1)} %channelize.3) | copy-start | bytes 12582916
  47.4 8.6 %copy-start.4 = (bf16[512,1024]{1,0:T(8,128)(2,1)S(1)}, bf16[512,1024]{1,0:T(8,128)(2,1)}, u32[]{:S(2)}) copy-start(bf16[512,1024]{1,0:T(8,128)(2,1)} %constant.17.clone.table_ref) | copy-start | bytes 3145732
  47.4 60.9 %all-to-all-start.1 = ((bf16[128,128,128]{2,1,0:T(8,128)(2,1)}), bf16[128,128,128]{2,1,0:T(8,128)(2,1)}, u32[]{:S(2)}, u32[]{:S(2)}) async-start(bf16[128,128,128]{2,1,0:T(8,128)(2,1)} %bitcast.8), calls=%async_computation.1 | async-start | bytes 8388608 | tf_op jit(solution)/shard_map/all_to_all | solution.py:173
  56.0 3.4 %copy-start.1 = (bf16[64,64,1024]{2,1,0:T(8,128)(2,1)S(1)}, bf16[64,64,1024]{2,1,0:T(8,128)(2,1)}, u32[]{:S(2)}) copy-start(bf16[64,64,1024]{2,1,0:T(8,128)(2,1)} %copy-done) | copy-start | bytes 25165828
  67.6 2.0 %copy-start.2 = (bf16[256,64,128]{2,1,0:T(8,128)(2,1)}, bf16[256,64,128]{2,1,0:T(8,128)(2,1)S(1)}, u32[]{:S(2)}) copy-start(bf16[256,64,128]{2,1,0:T(8,128)(2,1)S(1)} %channelize.2) | copy-start | bytes 12582916
  108.4 60.2 %all-to-all-start = ((bf16[128,128,128]{2,1,0:T(8,128)(2,1)}), bf16[128,128,128]{2,1,0:T(8,128)(2,1)}, u32[]{:S(2)}, u32[]{:S(2)}) async-start(bf16[128,128,128]{2,1,0:T(8,128)(2,1)} %bitcast.7), calls=%async_computation | async-start | bytes 8388608 | tf_op jit(solution)/shard_map/all_to_all | solution.py:173
where the time goes:
time: 177 us; the launch traced here: 176 us
  waiting for transfers between devices  93.9 us (53%)
  Pallas kernels  31.8 us (18%)
  other arithmetic  18.2 us (10%)
  starting transfers between devices  17.8 us (10%)
  local copies, waits for them, and re-layouts  14.4 us (8%)
    all_to_all x2, waiting for transfers between devices, on_device(): lax.all_to_all(parcel, ('inp', 'tm'), split_axis=0, concat_axis=0, tiled=...  83.7 us
    convert_element_type x1, other arithmetic, on_device(): filtered = filtered.astype(jnp.bfloat16)  18.2 us
    pallas_call x2, Pallas kernels, channelize(): pl.pallas_call(channelize_kernel, grid=(inputs // BLOCK,), in_specs=[pl.B...  16.4 us
    all_to_all x2, starting transfers between devices, on_device(): lax.all_to_all(parcel, ('inp', 'tm'), split_axis=0, concat_axis=0, tiled=...  15.9 us
    pallas_call x2, Pallas kernels, correlate(): pl.pallas_call(functools.partial(correlate_kernel, frames_all), grid=(eac...  15.4 us
    unnamed x13, local copies, waits for them, and re-layouts  11.7 us
    ppermute x1, waiting for transfers between devices, passed_along(): return lax.ppermute(array, axis, pairs)  10.2 us
  transfers between devices with their start and end apart: 3, of which 3 were waited for; matrix products, arithmetic and copies ran while one was open for 1% of the time, Pallas kernels for 9%

commit v1 on v0

--- a/solution.py
+++ b/solution.py
@@ -13,6 +13,7 @@
 TAPS = 4
 CHUNKS = 2
 BLOCK = 16
+LANES = 128
 SUB = 4
 
 
@@ -40,14 +41,37 @@
     return table.reshape(CHUNKS, 2 * groups * each, nfft)
 
 
-def channelize_kernel(table_ref, gain_ref, rows_ref, out_ref, turned):
-    inputs, frames, nfft = rows_ref.shape
+def filtered_rows(samples_ref, halo_ref, window, a):
+    nfft = samples_ref.shape[2]
+    columns = []
+    for start in range(0, nfft, LANES):
+        lanes = slice(start, start + LANES)
+        earlier = halo_ref[a, :, lanes].astype(jnp.float32)
+        unused = jnp.zeros((8 - earlier.shape[0], LANES), jnp.float32)
+        frames = samples_ref[a, :, lanes].astype(jnp.float32)
+        frames = jnp.concatenate([unused, earlier, frames], axis=0)
+        total = frames * window[0][:, lanes]
+        for tap in range(1, TAPS):
+            total = pltpu.roll(total, 1, 0) + frames * window[tap][:, lanes]
+        columns.append(total[8:].astype(jnp.bfloat16))
+    return jnp.concatenate(columns, axis=1)
+
+
+def channelize_kernel(table_ref, gain_ref, window_ref, halo_ref, samples_ref, out_ref, turned):
+    inputs, frames, nfft = samples_ref.shape
     count = table_ref.shape[0] // 2
     table = table_ref[...]
+    window = [window_ref[tap : tap + 1, :] for tap in range(TAPS)]
     lane = lax.broadcasted_iota(jnp.int32, (count, 2 * frames), 1)
     first = lane < frames
     for s in range(inputs // SUB):
-        rows = rows_ref[s * SUB : (s + 1) * SUB].reshape(SUB * frames, nfft)
+        rows = jnp.concatenate(
+            [
+                filtered_rows(samples_ref, halo_ref, window, a)
+                for a in range(s * SUB, (s + 1) * SUB)
+            ],
+            axis=0,
+        )
         both = lax.dot_general(
             table, rows, (((1,), (1,)), ((), ())), preferred_element_type=jnp.float32
         )
@@ -62,8 +86,8 @@
     out_ref[...] = turned[...].reshape(count, inputs, 2 * frames).astype(out_ref.dtype)
 
 
-def channelize(table, gain, filtered):
-    inputs, frames, nfft = filtered.shape
+def channelize(table, gain, window, halo, samples):
+    inputs, frames, nfft = samples.shape
     count = table.shape[0] // 2
     return pl.pallas_call(
         channelize_kernel,
@@ -71,10 +95,12 @@
         in_specs=[
             pl.BlockSpec(table.shape, lambda i: (0, 0)),
             pl.BlockSpec((1, count, BLOCK), lambda i: (i, 0, 0)),
+            pl.BlockSpec(window.shape, lambda i: (0, 0)),
+            pl.BlockSpec((BLOCK, TAPS - 1, nfft), lambda i: (i, 0, 0)),
             pl.BlockSpec((BLOCK, frames, nfft), lambda i: (i, 0, 0)),
         ],
         out_specs=pl.BlockSpec((count, BLOCK, 2 * frames), lambda i: (0, i, 0)),
-        out_shape=jax.ShapeDtypeStruct((count, inputs, 2 * frames), jnp.bfloat16),
+        out_shape=pltpu.HBM((count, inputs, 2 * frames), jnp.bfloat16),
         scratch_shapes=[pltpu.VMEM((count * BLOCK, 2 * frames), jnp.float32)],
         compiler_params=pltpu.CompilerParams(
             dimension_semantics=("arbitrary",), vmem_limit_bytes=40 * 2**20
@@ -85,7 +111,7 @@
             bytes_accessed=2 * (inputs * frames * nfft + count * inputs * 2 * frames),
         ),
         name="channelize",
-    )(table, gain, filtered)
+    )(table, gain, window, halo, pltpu.with_memory_space_constraint(samples, pltpu.HBM))
 
 
 def correlate_kernel(frames_all, blocks_ref, *refs):
@@ -153,14 +179,7 @@
     frames_all = n_time * local_frames
     tail = samples[:, local_frames - (TAPS - 1) :, :]
     before = passed_along(tail, "tm", 1)
-    padded = jnp.concatenate([before, samples], axis=1)
-    window = window_table(TAPS, nfft)
-    filtered = jnp.zeros((local_inputs, local_frames, nfft), jnp.float32)
-    for tap in range(TAPS):
-        filtered = filtered + window[tap] * padded[:, tap : tap + local_frames, :].astype(
-            jnp.float32
-        )
-    filtered = filtered.astype(jnp.bfloat16)
+    window = jnp.asarray(window_table(TAPS, nfft))
     tables = fourier_tables(channels, nfft, groups)
     gains = eq_gain.reshape(groups, CHUNKS, each, local_inputs // BLOCK, BLOCK)
     gains = gains.transpose(1, 3, 0, 2, 4).reshape(
@@ -168,7 +187,7 @@
     )
     visibilities = None
     for k in range(CHUNKS):
-        parcel = channelize(jnp.asarray(tables[k]), gains[k], filtered)
+        parcel = channelize(jnp.asarray(tables[k]), gains[k], window, before, samples)
         parcel = parcel.reshape(groups, each * local_inputs, 2 * local_frames)
         arrived = lax.all_to_all(
             parcel, ("inp", "tm"), split_axis=0, concat_axis=0, tiled=True

time: 177 us -> 163 us (0.921)
  other arithmetic: 18.2 us -> 0 us
  Pallas kernels: 31.8 us -> 49.4 us
  local copies, waits for them, and re-layouts: 14.4 us -> 4.59 us
  waiting for transfers between devices: 93.9 us -> 90.6 us
    convert_element_type x1 -> x0, other arithmetic: 18.2 us -> none  [on_device(): filtered = filtered.astype(jnp.bfloat16)]
    pallas_call x2, Pallas kernels: 16.4 us -> 34.1 us  [channelize(): pl.pallas_call(channelize_kernel, grid=(inputs // BLOCK,), in_specs=[pl.B...]
    unnamed x13 -> x7, local copies, waits for them, and re-layouts: 11.7 us -> 1.04 us
    all_to_all x2, waiting for transfers between devices: 83.7 us -> 80.2 us  [on_device(): lax.all_to_all(parcel, ('inp', 'tm'), split_axis=0, concat_axis=0, tiled=...]
  transfers between devices with their start and end apart: 3 -> 3, of which waited for: 3 -> 3; matrix products, arithmetic and copies ran while one was open for 1% -> 1% of each run, Pallas kernels for 9% -> 15%
where the time goes in v1:
time: 163 us
  waiting for transfers between devices  90.6 us (56%)
  Pallas kernels  49.4 us (30%)
  starting transfers between devices  17.8 us (11%)
  local copies, waits for them, and re-layouts  4.59 us (3%)
    all_to_all x2, waiting for transfers between devices, on_device(): lax.all_to_all(parcel, ('inp', 'tm'), split_axis=0, concat_axis=0, tiled=...  80.2 us
    pallas_call x2, Pallas kernels, channelize(): pl.pallas_call(channelize_kernel, grid=(inputs // BLOCK,), in_specs=[pl.B...  34.1 us
    all_to_all x2, starting transfers between devices, on_device(): lax.all_to_all(parcel, ('inp', 'tm'), split_axis=0, concat_axis=0, tiled=...  15.9 us
    pallas_call x2, Pallas kernels, correlate(): pl.pallas_call(functools.partial(correlate_kernel, frames_all), grid=(eac...  15.4 us
    ppermute x1, waiting for transfers between devices, passed_along(): return lax.ppermute(array, axis, pairs)  10.4 us
  transfers between devices with their start and end apart: 3, of which 3 were waited for; matrix products, arithmetic and copies ran while one was open for 1% of the time, Pallas kernels for 15%

profile of v1, /device:TPU:6, one launch (start us, length us, event | category | flops | bytes accessed | tf_op | source)
XLA Modules:
  0.0 162.5 jit_solution(8715716351516485040)
XLA Ops:
  0.0 0.0 copy-start.2
  0.0 0.0 copy-start.1
  0.0 2.4 %slice.12 = bf16[64,3,1024]{2,1,0:T(4,128)(2,1)} slice(bf16[64,64,1024]{2,1,0:T(8,128)(2,1)} %samples_ref.3), slice={[0:64], [61:64], [0:1024]} | slice | bytes 786432 | tf_op jit(solution)/shard_map/slice | solution.py:180
  2.4 1.9 %collective-permute-start = (bf16[64,3,1024]{2,1,0:T(4,128)(2,1)}, bf16[64,3,1024]{2,1,0:T(4,128)(2,1)S(1)}, u32[]{:S(2)}, u32[]{:S(2)}) collective-permute-start(bf16[64,3,1024]{2,1,0:T(4,128)(2,1)} %slice.12), channel_id=1, source_target_pairs={{0,1},{1,2},{2,3},{3,4},{4,5},{5,6},{6,7},{7,8},{8,9},{9,10},{10,1... | collective-permute-start | bytes 1179656 | tf_op jit(solution)/shard_map/ppermute | solution.py:23
  4.3 1.0 copy.8
  5.3 0.4 reshape.20
  5.8 0.2 fusion
  6.0 0.3 copy.10
  6.3 10.4 %collective-permute-done.halo_ref = bf16[64,3,1024]{2,1,0:T(4,128)(2,1)S(1)} collective-permute-done((bf16[64,3,1024]{2,1,0:T(4,128)(2,1)}, bf16[64,3,1024]{2,1,0:T(4,128)(2,1)S(1)}, u32[]{:S(2)}, u32[]{:S(2)}) %collective-permute-start) | collective-permute-done | bytes 393248 | tf_op jit(solution)/shard_map/ppermute | solution.py:23
  16.7 0.0 copy-done.2
  16.7 0.0 copy-done.1
  16.7 17.0 %channelize.3 = bf16[256,64,128]{2,1,0:T(8,128)(2,1)} custom-call(bf16[512,1024]{1,0:T(8,128)(2,1)S(1)} %copy-done.1, f32[4,256,16]{2,1,0:T(8,128)S(1)} %bitcast.7, f32[4,1024]{1,0:T(4,128)S(1)} %copy-done.2, bf16[64,3,1024]{2,1,0:T(4,128)(2,1)S(1)} %collective-permute-done.halo_ref, bf16[64,64,1024]{2,1,0:T(8,128)(2,1)} %samples_ref.3), custom_call_target="tpu_custom_call" | custom-call | flops 4294967296 | bytes 12582912 | tf_op jit(solution)/shard_map/channelize/pallas_call | solution.py:92
  33.7 0.0 copy-start
  33.7 8.3 %all-to-all-start.1 = ((bf16[128,128,128]{2,1,0:T(8,128)(2,1)}), bf16[128,128,128]{2,1,0:T(8,128)(2,1)}, u32[]{:S(2)}, u32[]{:S(2)}) async-start(bf16[128,128,128]{2,1,0:T(8,128)(2,1)} %bitcast.11), calls=%async_computation.1 | async-start | bytes 8388608 | tf_op jit(solution)/shard_map/all_to_all | solution.py:192
  42.0 0.3 copy.9
  42.3 0.0 copy-done
  42.3 17.1 %channelize.2 = bf16[256,64,128]{2,1,0:T(8,128)(2,1)} custom-call(bf16[512,1024]{1,0:T(8,128)(2,1)S(1)} %copy-done, f32[4,256,16]{2,1,0:T(8,128)S(1)} %bitcast.8, f32[4,1024]{1,0:T(4,128)S(1)} %copy-done.2, bf16[64,3,1024]{2,1,0:T(4,128)(2,1)S(1)} %collective-permute-done.halo_ref, bf16[64,64,1024]{2,1,0:T(8,128)(2,1)} %samples_ref.3), custom_call_target="tpu_custom_call" | custom-call | flops 4294967296 | bytes 12582912 | tf_op jit(solution)/shard_map/channelize/pallas_call | solution.py:92
  59.4 35.3 %all-to-all-done.1 = bf16[128,128,128]{2,1,0:T(8,128)(2,1)} async-done(((bf16[128,128,128]{2,1,0:T(8,128)(2,1)}), bf16[128,128,128]{2,1,0:T(8,128)(2,1)}, u32[]{:S(2)}, u32[]{:S(2)}) %all-to-all-start.1) | async-done | bytes 4194336 | tf_op jit(solution)/shard_map/all_to_all | solution.py:192
  94.6 7.6 %all-to-all-start = ((bf16[128,128,128]{2,1,0:T(8,128)(2,1)}), bf16[128,128,128]{2,1,0:T(8,128)(2,1)}, u32[]{:S(2)}, u32[]{:S(2)}) async-start(bf16[128,128,128]{2,1,0:T(8,128)(2,1)} %bitcast.10), calls=%async_computation | async-start | bytes 8388608 | tf_op jit(solution)/shard_map/all_to_all | solution.py:192
  102.2 7.7 %correlate.2.refs_0_ = f32[4,2,512,512]{3,2,1,0:T(8,128)} custom-call(bf16[8,16,2,64,128]{4,3,2,1,0:T(8,128)(2,1)} %bitcast.6.blocks_ref), custom_call_target="tpu_custom_call" | custom-call | flops 4294967296 | bytes 8388608 | tf_op jit(solution)/shard_map/correlate/pallas_call | solution.py:150
  109.9 44.9 %all-to-all-done = bf16[128,128,128]{2,1,0:T(8,128)(2,1)} async-done(((bf16[128,128,128]{2,1,0:T(8,128)(2,1)}), bf16[128,128,128]{2,1,0:T(8,128)(2,1)}, u32[]{:S(2)}, u32[]{:S(2)}) %all-to-all-start) | async-done | bytes 4194336 | tf_op jit(solution)/shard_map/all_to_all | solution.py:192
  154.8 7.7 %correlate.3 = f32[4,2,512,512]{3,2,1,0:T(8,128)} custom-call(bf16[8,16,2,64,128]{4,3,2,1,0:T(8,128)(2,1)} %bitcast.3.blocks_ref, f32[4,2,512,512]{3,2,1,0:T(8,128)} %correlate.2.refs_0_), custom_call_target="tpu_custom_call", output_to_operand_aliasing={{}: (1, {})} | custom-call | flops 4294967296 | bytes 8388608 | tf_op jit(solution)/shard_map/correlate/pallas_call | solution.py:150
Async XLA Ops:
  0.0 16.7 %copy-start.2 = (f32[4,1024]{1,0:T(4,128)S(1)}, f32[4,1024]{1,0:T(4,128)}, u32[]{:S(2)}) copy-start(f32[4,1024]{1,0:T(4,128)} %constant.6.clone.window_ref) | copy-start | bytes 49156
  0.0 16.7 %copy-start.1 = (bf16[512,1024]{1,0:T(8,128)(2,1)S(1)}, bf16[512,1024]{1,0:T(8,128)(2,1)}, u32[]{:S(2)}) copy-start(bf16[512,1024]{1,0:T(8,128)(2,1)} %constant.7.clone.table_ref) | copy-start | bytes 3145732
  2.4 14.3 %collective-permute-start = (bf16[64,3,1024]{2,1,0:T(4,128)(2,1)}, bf16[64,3,1024]{2,1,0:T(4,128)(2,1)S(1)}, u32[]{:S(2)}, u32[]{:S(2)}) collective-permute-start(bf16[64,3,1024]{2,1,0:T(4,128)(2,1)} %slice.12), channel_id=1, source_target_pairs={{0,1},{1,2},{2,3},{3,4},{4,5},{5,6},{6,7},{7,8},{8,9},{9,10},{10,1... | collective-permute-start | bytes 1179656 | tf_op jit(solution)/shard_map/ppermute | solution.py:23
  33.7 8.6 %copy-start = (bf16[512,1024]{1,0:T(8,128)(2,1)S(1)}, bf16[512,1024]{1,0:T(8,128)(2,1)}, u32[]{:S(2)}) copy-start(bf16[512,1024]{1,0:T(8,128)(2,1)} %constant.8.clone.table_ref) | copy-start | bytes 3145732
  33.7 60.9 %all-to-all-start.1 = ((bf16[128,128,128]{2,1,0:T(8,128)(2,1)}), bf16[128,128,128]{2,1,0:T(8,128)(2,1)}, u32[]{:S(2)}, u32[]{:S(2)}) async-start(bf16[128,128,128]{2,1,0:T(8,128)(2,1)} %bitcast.11), calls=%async_computation.1 | async-start | bytes 8388608 | tf_op jit(solution)/shard_map/all_to_all | solution.py:192
  94.6 60.2 %all-to-all-start = ((bf16[128,128,128]{2,1,0:T(8,128)(2,1)}), bf16[128,128,128]{2,1,0:T(8,128)(2,1)}, u32[]{:S(2)}, u32[]{:S(2)}) async-start(bf16[128,128,128]{2,1,0:T(8,128)(2,1)} %bitcast.10), calls=%async_computation | async-start | bytes 8388608 | tf_op jit(solution)/shard_map/all_to_all | solution.py:192

commit v2 on v0

v2 whole, which is shorter than its diff:
```python
import functools
import math

import jax
import jax.numpy as jnp
import ml_dtypes
import numpy as np
from jax import lax
from jax.experimental import pallas as pl
from jax.experimental.pallas import tpu as pltpu
from jax.sharding import PartitionSpec as P

TAPS = 4
LANES = 128
SUBLANES = 8
EARLY = 16
BLOCK = 16
SUB = 4
PITCH = 24
MIB = 2**20


def passed_along(array, axis, by):
    devices = lax.axis_size(axis)
    pairs = [(i, i + by) for i in range(devices) if 0 <= i + by < devices]
    return lax.ppermute(array, axis, pairs)


def window_table(taps, nfft):
    position = np.arange(taps * nfft, dtype=np.float64) + 0.5
    shape_part = np.sinc(position / nfft - taps / 2.0)
    taper = 0.5 - 0.5 * np.cos(position * (2.0 * math.pi / (taps * nfft)))
    return (shape_part * taper).reshape(taps, nfft).astype(np.float32)


def fourier_table(channels, nfft):
    phase = (np.arange(channels)[:, None] * np.arange(nfft)[None, :] % nfft) * (
        2.0 * math.pi / nfft
    )
    scale = 1.0 / math.sqrt(nfft)
    table = np.concatenate([np.cos(phase) * scale, -np.sin(phase) * scale])
    return table.astype(np.float32).astype(ml_dtypes.bfloat16)


def summed_taps(frames, window):
    earlier = pltpu.roll(frames, 2, 0)
    odd = frames * window[2] + earlier * window[0]
    return frames * window[3] + earlier * window[1] + pltpu.roll(odd, 1, 0)


def filter_late_kernel(window_ref, samples_ref, out_ref):
    inputs, frames, nfft = samples_ref.shape
    for start in range(0, nfft, LANES):
        lanes = slice(start, start + LANES)
        window = [window_ref[tap : tap + 1, lanes] for tap in range(TAPS)]
        for a in range(inputs):
            known = samples_ref[a, EARLY - SUBLANES :, lanes].astype(jnp.float32)
            total = summed_taps(known, window)
            out_ref[a, :, lanes] = total[SUBLANES:].astype(out_ref.dtype)


def filter_early_kernel(window_ref, halo_ref, samples_ref, out_ref):
    inputs, frames, nfft = samples_ref.shape
    unused = jnp.zeros((SUBLANES - (TAPS - 1), LANES), jnp.float32)
    for start in range(0, nfft, LANES):
        lanes = slice(start, start + LANES)
        window = [window_ref[tap : tap + 1, lanes] for tap in range(TAPS)]
        for a in range(inputs):
            halo = halo_ref[a, :, lanes].astype(jnp.float32)
            known = samples_ref[a, :, lanes].astype(jnp.float32)
            known = jnp.concatenate([unused, halo, known], axis=0)
            total = summed_taps(known, window)
            out_ref[a, :, lanes] = total[SUBLANES:].astype(out_ref.dtype)


def filter_late(window, samples):
    inputs, frames, nfft = samples.shape
    return pl.pallas_call(
        filter_late_kernel,
        grid=(inputs // BLOCK,),
        in_specs=[
            pl.BlockSpec(window.shape, lambda i: (0, 0)),
            pl.BlockSpec((BLOCK, frames, nfft), lambda i: (i, 0, 0)),
        ],
        out_specs=pl.BlockSpec((BLOCK, frames - EARLY, nfft), lambda i: (i, 0, 0)),
        out_shape=jax.ShapeDtypeStruct((inputs, frames - EARLY, nfft), jnp.bfloat16),
        compiler_params=pltpu.CompilerParams(
            dimension_semantics=("arbitrary",), vmem_limit_bytes=16 * MIB
        ),
        cost_estimate=pl.CostEstimate(
            flops=2 * TAPS * inputs * (frames - EARLY) * nfft,
            transcendentals=0,
            bytes_accessed=2 * inputs * (2 * frames - EARLY) * nfft,
        ),
        name="filter_late",
    )(window, samples)


def filter_early(window, halo, samples):
    inputs, frames, nfft = samples.shape
    return pl.pallas_call(
        filter_early_kernel,
        grid=(inputs // BLOCK,),
        in_specs=[
            pl.BlockSpec(window.shape, lambda i: (0, 0)),
            pl.BlockSpec((BLOCK, TAPS - 1, nfft), lambda i: (i, 0, 0)),
            pl.BlockSpec((BLOCK, EARLY, nfft), lambda i: (i, 0, 0)),
        ],
        out_specs=pl.BlockSpec((BLOCK, EARLY, nfft), lambda i: (i, 0, 0)),
        out_shape=jax.ShapeDtypeStruct((inputs, EARLY, nfft), jnp.bfloat16),
        compiler_params=pltpu.CompilerParams(
            dimension_semantics=("arbitrary",), vmem_limit_bytes=16 * MIB
        ),
        cost_estimate=pl.CostEstimate(
            flops=2 * TAPS * inputs * EARLY * nfft,
            transcendentals=0,
            bytes_accessed=4 * inputs * EARLY * nfft,
        ),
        name="filter_early",
    )(window, halo, samples)


def channelize_kernel(table_ref, gain_ref, early_ref, late_ref, out_ref, turned):
    inputs, _, nfft = late_ref.shape
    frames = early_ref.shape[1] + late_ref.shape[1]
    count = table_ref.shape[0] // 2
    table = table_ref[...]
    gain = jnp.transpose(gain_ref[...])
    lane = lax.broadcasted_iota(jnp.int32, (count, 2 * frames), 1)
    first = lane < frames
    for s in range(inputs // SUB):
        rows = []
        for a in range(s * SUB, (s + 1) * SUB):
            rows += [early_ref[a], late_ref[a]]
        both = lax.dot_general(
            table,
            jnp.concatenate(rows, axis=0),
            (((1,), (1,)), ((), ())),
            preferred_element_type=jnp.float32,
        )
        for j in range(SUB // 2):
            real = both[:count, j * 2 * frames : (j + 1) * 2 * frames]
            imag = both[count:, j * 2 * frames : (j + 1) * 2 * frames]
            even = jnp.where(first, real, pltpu.roll(imag, frames, 1))
            odd = jnp.where(first, pltpu.roll(real, frames, 1), imag)
            a = s * SUB + 2 * j
            turned[pl.ds(a, count, stride=PITCH), :] = even * gain[:, a : a + 1]
            turned[pl.ds(a + 1, count, stride=PITCH), :] = odd * gain[:, a + 1 : a + 2]
    spectra = turned[...].reshape(count, PITCH, 2 * frames)
    out_ref[...] = spectra[:, :inputs].astype(out_ref.dtype)


def channelize(table, gain, early, late):
    inputs, late_frames, nfft = late.shape
    frames = EARLY + late_frames
    count = table.shape[0] // 2
    return pl.pallas_call(
        channelize_kernel,
        grid=(inputs // BLOCK,),
        in_specs=[
            pl.BlockSpec(table.shape, lambda i: (0, 0)),
            pl.BlockSpec((BLOCK, count), lambda i: (i, 0)),
            pl.BlockSpec((BLOCK, EARLY, nfft), lambda i: (i, 0, 0)),
            pl.BlockSpec((BLOCK, late_frames, nfft), lambda i: (i, 0, 0)),
        ],
        out_specs=pl.BlockSpec((count, BLOCK, 2 * frames), lambda i: (0, i, 0)),
        out_shape=pltpu.HBM((count, inputs, 2 * frames), jnp.bfloat16),
        scratch_shapes=[pltpu.VMEM((count * PITCH, 2 * frames), jnp.float32)],
        compiler_params=pltpu.CompilerParams(
            dimension_semantics=("arbitrary",), vmem_limit_bytes=32 * MIB
        ),
        cost_estimate=pl.CostEstimate(
            flops=4 * count * inputs * frames * nfft,
            transcendentals=0,
            bytes_accessed=2 * (inputs * frames * nfft + count * inputs * 2 * frames),
        ),
        name="channelize",
    )(table, gain, early, late)


def correlate_kernel(frames_all, blocks_ref, out_ref):
    n_time = blocks_ref.shape[1]
    inputs_all = blocks_ref.shape[0] * blocks_ref.shape[3]
    width = blocks_ref.shape[4]
    half = width // 2
    straight, crossed = [], []
    for t in range(n_time):
        part = blocks_ref[:, t, 0].reshape(inputs_all, width)
        straight.append(part)
        crossed.append(jnp.concatenate([part[:, half:], -part[:, :half]], axis=1))
    straight = jnp.concatenate(straight, axis=1)
    crossed = jnp.concatenate(crossed, axis=1)
    last = (((1,), (1,)), ((), ()))
    scale = 1.0 / frames_all
    low, high = slice(0, inputs_all // 2), slice(inputs_all // 2, inputs_all)
    for rows, columns in ((low, low), (high, low), (high, high)):
        for k, left in enumerate((straight, crossed)):
            product = scale * lax.dot_general(
                left[rows], straight[columns], last, preferred_element_type=jnp.float32
            )
            out_ref[0, k, rows, columns] = product
            if rows != columns:
                mirrored = product.T
                out_ref[0, k, columns, rows] = mirrored if k == 0 else -mirrored


def correlate(arrived, frames_all):
    n_inp, n_time, chan_dev, local, width = arrived.shape
    inputs_all = n_inp * local
    return pl.pallas_call(
        functools.partial(correlate_kernel, frames_all),
        grid=(chan_dev,),
        in_specs=[pl.BlockSpec((n_inp, n_time, 1, local, width), lambda i: (0, 0, i, 0, 0))],
        out_specs=pl.BlockSpec((1, 2, inputs_all, inputs_all), lambda i: (i, 0, 0, 0)),
        out_shape=jax.ShapeDtypeStruct((chan_dev, 2, inputs_all, inputs_all), jnp.float32),
        compiler_params=pltpu.CompilerParams(
            dimension_semantics=("arbitrary",), vmem_limit_bytes=40 * MIB
        ),
        cost_estimate=pl.CostEstimate(
            flops=chan_dev * 3 * inputs_all * inputs_all * n_time * width,
            transcendentals=0,
            bytes_accessed=chan_dev
            * (2 * inputs_all * n_time * width + 8 * inputs_all * inputs_all),
        ),
        name="correlate",
    )(arrived)


def on_device(samples, eq_gain):
    local_inputs, local_frames, nfft = samples.shape
    channels = nfft // 2
    n_inp = lax.axis_size("inp")
    n_time = lax.axis_size("tm")
    groups = n_inp * n_time
    chan_dev = channels // groups
    frames_all = n_time * local_frames
    tail = samples[:, local_frames - (TAPS - 1) :, :]
    halo = passed_along(tail, "tm", 1)
    window = jnp.asarray(window_table(TAPS, nfft))
    table = jnp.asarray(fourier_table(channels, nfft))
    samples = pltpu.with_memory_space_constraint(samples, pltpu.HBM)
    late = filter_late(window, samples)
    early = filter_early(window, halo, samples)
    parcel = channelize(table, eq_gain.T, early, late)
    parcel = parcel.reshape(groups, chan_dev * local_inputs, 2 * local_frames)
    arrived = lax.all_to_all(parcel, ("inp", "tm"), split_axis=0, concat_axis=0, tiled=True)
    arrived = arrived.reshape(n_inp, n_time, chan_dev, local_inputs, 2 * local_frames)
    return correlate(arrived, frames_all)


def solution(mesh):
    placed = (P("inp", "tm", None), P(None, "inp"))
    return jax.shard_map(
        on_device,
        mesh=mesh,
        in_specs=placed,
        out_specs=P(("inp", "tm"), None, None, None),
        check_vma=False,
    )
```

time: 177 us -> 150 us (0.85)
  blocking collectives: 0 us -> 107 us
  waiting for transfers between devices: 93.9 us -> 3.87 us
  other arithmetic: 18.2 us -> 0 us
  starting transfers between devices: 17.8 us -> 1.92 us
  local copies, waits for them, and re-layouts: 14.4 us -> 2.22 us
  Pallas kernels: 31.8 us -> 34.4 us
    all_to_all x0 -> x1, blocking collectives: none -> 107 us  [on_device(): lax.all_to_all(parcel, ('inp', 'tm'), split_axis=0, concat_axis=0, tiled=...]
    all_to_all x2 -> x0, waiting for transfers between devices: 83.7 us -> none  [on_device(): lax.all_to_all(parcel, ('inp', 'tm'), split_axis=0, concat_axis=0, tiled=...]
    convert_element_type x1 -> x0, other arithmetic: 18.2 us -> none  [on_device(): filtered = filtered.astype(jnp.bfloat16)]
    all_to_all x2 -> x0, starting transfers between devices: 15.9 us -> none  [on_device(): lax.all_to_all(parcel, ('inp', 'tm'), split_axis=0, concat_axis=0, tiled=...]
    unnamed x13 -> x6, local copies, waits for them, and re-layouts: 11.7 us -> 0.73 us
    ppermute x1, waiting for transfers between devices: 10.2 us -> 3.87 us  [passed_along(): return lax.ppermute(array, axis, pairs)]
    pallas_call x2 -> x3, Pallas kernels: 15.4 us -> 20.8 us  [the longest x1 9.27 us: correlate(): pl.pallas_call(functools.partial(correlate_kernel, frames_all), grid=(cha...]
    pallas_call x2 -> x1, Pallas kernels: 16.4 us -> 13.6 us  [channelize(): pl.pallas_call(channelize_kernel, grid=(inputs // BLOCK,), in_specs=[pl.B...]
  transfers between devices with their start and end apart: 3 -> 1, of which waited for: 3 -> 1; matrix products, arithmetic and copies ran while one was open for 1% -> 0% of each run, Pallas kernels for 9% -> 5%
where the time goes in v2:
time: 150 us
  blocking collectives  107 us (71%)
  Pallas kernels  34.4 us (23%)
  waiting for transfers between devices  3.87 us (3%)
  local copies, waits for them, and re-layouts  2.22 us (1%)
  starting transfers between devices  1.92 us (1%)
    all_to_all x1, blocking collectives, on_device(): lax.all_to_all(parcel, ('inp', 'tm'), split_axis=0, concat_axis=0, tiled=...  107 us
    pallas_call x1, Pallas kernels, channelize(): pl.pallas_call(channelize_kernel, grid=(inputs // BLOCK,), in_specs=[pl.B...  13.6 us
    pallas_call x1, Pallas kernels, correlate(): pl.pallas_call(functools.partial(correlate_kernel, frames_all), grid=(cha...  9.27 us
    pallas_call x1, Pallas kernels, filter_late(): pl.pallas_call(filter_late_kernel, grid=(inputs // BLOCK,), in_specs=[pl....  7.56 us
    pallas_call x1, Pallas kernels, filter_early(): pl.pallas_call(filter_early_kernel, grid=(inputs // BLOCK,), in_specs=[pl...  3.96 us
    ppermute x1, waiting for transfers between devices, passed_along(): return lax.ppermute(array, axis, pairs)  3.87 us
  transfers between devices with their start and end apart: 1, of which 1 were waited for; matrix products, arithmetic and copies ran while one was open for 0% of the time, Pallas kernels for 5%

profile of v2, /device:TPU:6, one launch (start us, length us, event | category | flops | bytes accessed | tf_op | source)
XLA Modules:
  0.0 149.9 jit_solution(6118404065519722469)
XLA Ops:
  0.0 1.5 slice.3
  1.5 1.9 %collective-permute-start = (bf16[64,3,1024]{2,1,0:T(4,128)(2,1)S(1)}, bf16[64,3,1024]{2,1,0:T(4,128)(2,1)S(1)}, u32[]{:S(2)}, u32[]{:S(2)}) collective-permute-start(bf16[64,3,1024]{2,1,0:T(4,128)(2,1)S(1)} %slice.3), channel_id=1, source_target_pairs={{0,1},{1,2},{2,3},{3,4},{4,5},{5,6},{6,7},{7,8},{8,9},{9,10},{10,1... | collective-permute-start | bytes 1179656 | tf_op jit(solution)/shard_map/ppermute | solution.py:26
  3.4 0.0 copy-start
  3.4 0.7 copy-done
  4.2 7.6 %filter_late.1.late_ref = bf16[64,48,1024]{2,1,0:T(8,128)(2,1)S(1)} custom-call(f32[4,1024]{1,0:T(4,128)S(1)} %copy-done, bf16[64,64,1024]{2,1,0:T(8,128)(2,1)} %samples_ref.3), custom_call_target="tpu_custom_call" | custom-call | flops 25165824 | bytes 14680064 | tf_op jit(solution)/shard_map/filter_late/pallas_call | solution.py:78
  11.7 0.0 copy-start.1
  11.7 0.0 copy-start.2
  11.7 3.9 %collective-permute-done.halo_ref = bf16[64,3,1024]{2,1,0:T(4,128)(2,1)S(1)} collective-permute-done((bf16[64,3,1024]{2,1,0:T(4,128)(2,1)S(1)}, bf16[64,3,1024]{2,1,0:T(4,128)(2,1)S(1)}, u32[]{:S(2)}, u32[]{:S(2)}) %collective-permute-start) | collective-permute-done | bytes 393248 | tf_op jit(solution)/shard_map/ppermute | solution.py:26
  15.6 4.0 %filter_early.1.early_ref = bf16[64,16,1024]{2,1,0:T(8,128)(2,1)S(1)} custom-call(f32[4,1024]{1,0:T(4,128)S(1)} %copy-done, bf16[64,3,1024]{2,1,0:T(4,128)(2,1)S(1)} %collective-permute-done.halo_ref, bf16[64,64,1024]{2,1,0:T(8,128)(2,1)} %samples_ref.3), custom_call_target="tpu_custom_call" | custom-call | flops 8388608 | bytes 4194304 | tf_op jit(solution)/shard_map/filter_early/pallas_call | solution.py:101
  19.6 0.0 copy-done.1
  19.6 0.0 copy-done.2
  19.6 13.6 %channelize.1 = bf16[512,64,128]{2,1,0:T(8,128)(2,1)} custom-call(bf16[1024,1024]{1,0:T(8,128)(2,1)S(1)} %copy-done.2, f32[64,512]{1,0:T(8,128)S(1)} %bitcast.4, bf16[64,16,1024]{2,1,0:T(8,128)(2,1)S(1)} %filter_early.1.early_ref, bf16[64,48,1024]{2,1,0:T(8,128)(2,1)S(1)} %filter_late.1.late_ref), custom_call_target="tpu_custom_call" | custom-call | flops 8589934592 | bytes 16777216 | tf_op jit(solution)/shard_map/channelize/pallas_call | solution.py:157
  33.2 107.4 %all_to_all.5 = bf16[128,256,128]{2,1,0:T(8,128)(2,1)S(1)} all-to-all(bf16[128,256,128]{2,1,0:T(8,128)(2,1)} %bitcast.5), channel_id=1, replica_groups=mesh['inp'=8,'tm'=16] {'inp','tm'}, dimensions={0} | all-to-all | bytes 16777216 | tf_op jit(solution)/shard_map/all_to_all | solution.py:246
  140.6 9.3 %correlate.1 = f32[4,2,512,512]{3,2,1,0:T(8,128)} custom-call(bf16[8,16,4,64,128]{4,3,2,1,0:T(8,128)(2,1)S(1)} %bitcast.3), custom_call_target="tpu_custom_call" | custom-call | flops 6442450944 | bytes 16777216 | tf_op jit(solution)/shard_map/correlate/pallas_call | solution.py:210
Async XLA Ops:
  1.5 14.1 %collective-permute-start = (bf16[64,3,1024]{2,1,0:T(4,128)(2,1)S(1)}, bf16[64,3,1024]{2,1,0:T(4,128)(2,1)S(1)}, u32[]{:S(2)}, u32[]{:S(2)}) collective-permute-start(bf16[64,3,1024]{2,1,0:T(4,128)(2,1)S(1)} %slice.3), channel_id=1, source_target_pairs={{0,1},{1,2},{2,3},{3,4},{4,5},{5,6},{6,7},{7,8},{8,9},{9,10},{10,1... | collective-permute-start | bytes 1179656 | tf_op jit(solution)/shard_map/ppermute | solution.py:26
  3.4 0.7 copy-start
  11.7 7.9 %copy-start.1 = (f32[512,64]{0,1:T(8,128)S(1)}, f32[512,64]{0,1:T(8,128)}, u32[]{:S(2)}) copy-start(f32[512,64]{0,1:T(8,128)} %param.5) | copy-start | bytes 393220
  11.7 7.9 %copy-start.2 = (bf16[1024,1024]{1,0:T(8,128)(2,1)S(1)}, bf16[1024,1024]{1,0:T(8,128)(2,1)}, u32[]{:S(2)}) copy-start(bf16[1024,1024]{1,0:T(8,128)(2,1)} %constant.5.clone.table_ref) | copy-start | bytes 6291460

commit v3 on v2

v3 whole, which is shorter than its diff:
```python
import functools
import math

import jax
import jax.numpy as jnp
import ml_dtypes
import numpy as np
from jax import lax
from jax.experimental import pallas as pl
from jax.experimental.pallas import tpu as pltpu
from jax.sharding import PartitionSpec as P

TAPS = 4
LANES = 128
SUBLANES = 8
BLOCK = 16
PAIRS = 8
SUB = 2
PITCH = 2 * PAIRS + 1
MIB = 2**20


def passed_along(array, axis, by):
    devices = lax.axis_size(axis)
    pairs = [(i, i + by) for i in range(devices) if 0 <= i + by < devices]
    return lax.ppermute(array, axis, pairs)


def window_table(taps, nfft):
    position = np.arange(taps * nfft, dtype=np.float64) + 0.5
    shape_part = np.sinc(position / nfft - taps / 2.0)
    taper = 0.5 - 0.5 * np.cos(position * (2.0 * math.pi / (taps * nfft)))
    return (shape_part * taper).reshape(taps, nfft).astype(np.float32)


def fourier_tables(channels, nfft):
    phase = (np.arange(channels)[:, None] * np.arange(nfft // 2)[None, :] % nfft) * (
        2.0 * math.pi / nfft
    )
    scale = 1.0 / math.sqrt(nfft)
    table = np.stack([np.cos(phase) * scale, -np.sin(phase) * scale])
    table = table.astype(np.float32).astype(ml_dtypes.bfloat16)
    table = table.reshape(2, channels // 2, 2, nfft // 2).transpose(2, 0, 1, 3)
    return table.reshape(2, channels, nfft // 2)


def summed_taps(frames, window_ref, lanes):
    window = [window_ref[tap : tap + 1, lanes] for tap in range(TAPS)]
    earlier = pltpu.roll(frames, 2, 0)
    odd = frames * window[2] + earlier * window[0]
    return frames * window[3] + earlier * window[1] + pltpu.roll(odd, 1, 0)


def folded(rows_of, window_ref, store, nfft):
    for start in range(0, nfft // 2, LANES):
        near = slice(start, start + LANES)
        far = slice(nfft // 2 + start, nfft // 2 + start + LANES)
        one = summed_taps(rows_of(near), window_ref, near)[SUBLANES:]
        two = summed_taps(rows_of(far), window_ref, far)[SUBLANES:]
        store(near, one + two)
        store(far, one - two)


def filter_late_kernel(window_ref, samples_ref, out_ref):
    inputs, frames, nfft = samples_ref.shape
    for a in range(inputs):

        def rows_of(lanes):
            return samples_ref[a, :, lanes].astype(jnp.float32)

        def store(lanes, rows):
            out_ref[a, SUBLANES:, lanes] = rows.astype(out_ref.dtype)

        folded(rows_of, window_ref, store, nfft)


def filter_early_kernel(window_ref, halo_ref, samples_ref, late_ref, out_ref):
    inputs, frames, nfft = samples_ref.shape
    unused = jnp.zeros((SUBLANES - (TAPS - 1), LANES), jnp.float32)
    for a in range(inputs):

        def rows_of(lanes):
            halo = halo_ref[a, :, lanes].astype(jnp.float32)
            known = samples_ref[a, :, lanes].astype(jnp.float32)
            return jnp.concatenate([unused, halo, known], axis=0)

        def store(lanes, rows):
            out_ref[a, :, lanes] = rows.astype(out_ref.dtype)

        folded(rows_of, window_ref, store, nfft)


def filter_late(window, samples):
    inputs, frames, nfft = samples.shape
    return pl.pallas_call(
        filter_late_kernel,
        grid=(inputs // BLOCK,),
        in_specs=[
            pl.BlockSpec(window.shape, lambda i: (0, 0)),
            pl.BlockSpec((BLOCK, frames, nfft), lambda i: (i, 0, 0)),
        ],
        out_specs=pl.BlockSpec((BLOCK, frames, nfft), lambda i: (i, 0, 0)),
        out_shape=jax.ShapeDtypeStruct((inputs, frames, nfft), jnp.bfloat16),
        compiler_params=pltpu.CompilerParams(
            dimension_semantics=("arbitrary",), vmem_limit_bytes=16 * MIB
        ),
        cost_estimate=pl.CostEstimate(
            flops=2 * TAPS * inputs * frames * nfft,
            transcendentals=0,
            bytes_accessed=4 * inputs * frames * nfft,
        ),
        name="filter_late",
    )(window, samples)


def filter_early(window, halo, samples, late):
    inputs, frames, nfft = samples.shape
    return pl.pallas_call(
        filter_early_kernel,
        grid=(inputs // BLOCK,),
        in_specs=[
            pl.BlockSpec(window.shape, lambda i: (0, 0)),
            pl.BlockSpec((BLOCK, TAPS - 1, nfft), lambda i: (i, 0, 0)),
            pl.BlockSpec((BLOCK, SUBLANES, nfft), lambda i: (i, 0, 0)),
            pl.BlockSpec(memory_space=pl.ANY),
        ],
        out_specs=pl.BlockSpec((BLOCK, SUBLANES, nfft), lambda i: (i, 0, 0)),
        out_shape=jax.ShapeDtypeStruct((inputs, frames, nfft), jnp.bfloat16),
        input_output_aliases={3: 0},
        compiler_params=pltpu.CompilerParams(
            dimension_semantics=("arbitrary",), vmem_limit_bytes=16 * MIB
        ),
        cost_estimate=pl.CostEstimate(
            flops=2 * TAPS * inputs * SUBLANES * nfft,
            transcendentals=0,
            bytes_accessed=4 * inputs * SUBLANES * nfft,
        ),
        name="filter_early",
    )(window, halo, samples, late)


def channelize_kernel(table_ref, gain_ref, rows_ref, out_ref, turned, gains):
    _, pairs, frames, nfft = rows_ref.shape
    depth = nfft // 2
    count = table_ref.shape[1] // 2
    lane = lax.broadcasted_iota(jnp.int32, (count, 2 * frames), 1)
    first = lane < frames
    unused = jnp.zeros((LANES - 2 * pairs, 2 * count), jnp.float32)
    gains[...] = jnp.transpose(jnp.concatenate([gain_ref[0], gain_ref[1], unused], axis=0))
    for parity in range(2):
        gain = gains[pl.ds(parity, count, stride=2), :]
        columns = slice(parity * depth, (parity + 1) * depth)
        for s in range(0, pairs, SUB):
            rows = [rows_ref[h, i, :, columns] for i in range(s, s + SUB) for h in range(2)]
            both = lax.dot_general(
                table_ref[parity],
                jnp.concatenate(rows, axis=0),
                (((1,), (1,)), ((), ())),
                preferred_element_type=jnp.float32,
            )
            for i in range(s, s + SUB):
                lanes = slice((i - s) * 2 * frames, (i - s + 1) * 2 * frames)
                scale = jnp.where(first, gain[:, i : i + 1], gain[:, pairs + i : pairs + i + 1])
                start = parity * count * PITCH + i
                turned[pl.ds(start, count, stride=PITCH), :] = both[:count, lanes] * scale
                turned[pl.ds(start + pairs, count, stride=PITCH), :] = both[count:, lanes] * scale
    for parity in range(2):
        for c in range(count):
            start = (parity * count + c) * PITCH
            for r in range(2):
                rows = turned[start + r * pairs : start + (r + 1) * pairs, :]
                out_ref[2 * c + parity, r] = rows.astype(out_ref.dtype)


def channelize(tables, gain, rows):
    inputs, frames, nfft = rows.shape
    channels = tables.shape[1]
    half = inputs // 2
    return pl.pallas_call(
        channelize_kernel,
        grid=(half // PAIRS,),
        in_specs=[
            pl.BlockSpec(tables.shape, lambda i: (0, 0, 0)),
            pl.BlockSpec((2, PAIRS, channels), lambda i: (0, i, 0)),
            pl.BlockSpec((2, PAIRS, frames, nfft), lambda i: (0, i, 0, 0)),
        ],
        out_specs=pl.BlockSpec((channels, 2, PAIRS, 2 * frames), lambda i: (0, 0, i, 0)),
        out_shape=pltpu.HBM((channels, 2, half, 2 * frames), jnp.bfloat16),
        scratch_shapes=[
            pltpu.VMEM((channels * PITCH, 2 * frames), jnp.float32),
            pltpu.VMEM((channels, LANES), jnp.float32),
        ],
        compiler_params=pltpu.CompilerParams(
            dimension_semantics=("arbitrary",), vmem_limit_bytes=32 * MIB
        ),
        cost_estimate=pl.CostEstimate(
            flops=2 * channels * inputs * frames * nfft,
            transcendentals=0,
            bytes_accessed=2 * (inputs * frames * nfft + channels * inputs * 2 * frames),
        ),
        name="channelize",
    )(tables, gain.reshape(2, half, channels), rows.reshape(2, half, frames, nfft))


def correlate_kernel(frames_all, blocks_ref, out_ref):
    n_time = blocks_ref.shape[1]
    inputs_all = blocks_ref.shape[0] * blocks_ref.shape[3]
    width = blocks_ref.shape[4]
    half = width // 2
    n_inp, pairs = blocks_ref.shape[0], blocks_ref.shape[3] // 2
    first = lax.broadcasted_iota(jnp.int32, (n_inp, pairs, width), 2) < half
    straight, crossed = [], []
    for t in range(n_time):
        real, imag = blocks_ref[:, t, 0, :pairs], blocks_ref[:, t, 0, pairs:]
        real_turned = jnp.concatenate([real[..., half:], real[..., :half]], axis=2)
        imag_turned = jnp.concatenate([imag[..., half:], imag[..., :half]], axis=2)
        low_rows = jnp.where(first, real, imag_turned)
        high_rows = jnp.where(first, real_turned, imag)
        rows = jnp.concatenate([low_rows, high_rows], axis=1)
        straight.append(rows.reshape(inputs_all, width))
        low_rows = jnp.where(first, imag, -real_turned)
        high_rows = jnp.where(first, imag_turned, -real)
        rows = jnp.concatenate([low_rows, high_rows], axis=1)
        crossed.append(rows.reshape(inputs_all, width))
    straight = jnp.concatenate(straight, axis=1)
    crossed = jnp.concatenate(crossed, axis=1)
    last = (((1,), (1,)), ((), ()))
    scale = 1.0 / frames_all
    low, high = slice(0, inputs_all // 2), slice(inputs_all // 2, inputs_all)
    for rows, columns in ((low, low), (high, low), (high, high)):
        for k, left in enumerate((straight, crossed)):
            product = scale * lax.dot_general(
                left[rows], straight[columns], last, preferred_element_type=jnp.float32
            )
            out_ref[0, k, rows, columns] = product
            if rows != columns:
                mirrored = product.T
                out_ref[0, k, columns, rows] = mirrored if k == 0 else -mirrored


def correlate(arrived, frames_all):
    n_inp, n_time, chan_dev, local, width = arrived.shape
    inputs_all = n_inp * local
    return pl.pallas_call(
        functools.partial(correlate_kernel, frames_all),
        grid=(chan_dev,),
        in_specs=[pl.BlockSpec((n_inp, n_time, 1, local, width), lambda i: (0, 0, i, 0, 0))],
        out_specs=pl.BlockSpec((1, 2, inputs_all, inputs_all), lambda i: (i, 0, 0, 0)),
        out_shape=jax.ShapeDtypeStruct((chan_dev, 2, inputs_all, inputs_all), jnp.float32),
        compiler_params=pltpu.CompilerParams(
            dimension_semantics=("arbitrary",), vmem_limit_bytes=40 * MIB
        ),
        cost_estimate=pl.CostEstimate(
            flops=chan_dev * 3 * inputs_all * inputs_all * n_time * width,
            transcendentals=0,
            bytes_accessed=chan_dev
            * (2 * inputs_all * n_time * width + 8 * inputs_all * inputs_all),
        ),
        name="correlate",
    )(arrived)


def on_device(samples, eq_gain):
    local_inputs, local_frames, nfft = samples.shape
    channels = nfft // 2
    n_inp = lax.axis_size("inp")
    n_time = lax.axis_size("tm")
    groups = n_inp * n_time
    chan_dev = channels // groups
    frames_all = n_time * local_frames
    tail = samples[:, local_frames - (TAPS - 1) :, :]
    halo = passed_along(tail, "tm", 1)
    window = jnp.asarray(window_table(TAPS, nfft))
    tables = jnp.asarray(fourier_tables(channels, nfft))
    samples = pltpu.with_memory_space_constraint(samples, pltpu.HBM)
    late = filter_late(window, samples)
    rows = filter_early(window, halo, samples, late)
    parcel = channelize(tables, eq_gain.T, rows)
    parcel = parcel.reshape(groups, chan_dev * local_inputs, 2 * local_frames)
    arrived = lax.all_to_all(parcel, ("inp", "tm"), split_axis=0, concat_axis=0, tiled=True)
    arrived = arrived.reshape(n_inp, n_time, chan_dev, local_inputs, 2 * local_frames)
    return correlate(arrived, frames_all)


def solution(mesh):
    placed = (P("inp", "tm", None), P(None, "inp"))
    return jax.shard_map(
        on_device,
        mesh=mesh,
        in_specs=placed,
        out_specs=P(("inp", "tm"), None, None, None),
        check_vma=False,
    )
```

time: 150 us -> 145 us (0.967)
  Pallas kernels: 34.4 us -> 29.7 us
    pallas_call x1, Pallas kernels: 13.6 us -> 8.16 us  [channelize(): pl.pallas_call(channelize_kernel, grid=(half // PAIRS,), in_specs=[pl.Blo...]
  transfers between devices with their start and end apart: 1 -> 1, of which waited for: 1 -> 1; matrix products, arithmetic and copies ran while one was open for 0% -> 0% of each run, Pallas kernels for 5% -> 6%
where the time goes in v3:
time: 145 us
  blocking collectives  108 us (74%)
  Pallas kernels  29.7 us (20%)
  waiting for transfers between devices  2.69 us (2%)
  local copies, waits for them, and re-layouts  2.22 us (2%)
  starting transfers between devices  1.92 us (1%)
    all_to_all x1, blocking collectives, on_device(): lax.all_to_all(parcel, ('inp', 'tm'), split_axis=0, concat_axis=0, tiled=...  108 us
    pallas_call x1, Pallas kernels, correlate(): pl.pallas_call(functools.partial(correlate_kernel, frames_all), grid=(cha...  9.62 us
    pallas_call x1, Pallas kernels, filter_late(): pl.pallas_call(filter_late_kernel, grid=(inputs // BLOCK,), in_specs=[pl....  8.74 us
    pallas_call x1, Pallas kernels, channelize(): pl.pallas_call(channelize_kernel, grid=(half // PAIRS,), in_specs=[pl.Blo...  8.16 us
    pallas_call x1, Pallas kernels, filter_early(): pl.pallas_call(filter_early_kernel, grid=(inputs // BLOCK,), in_specs=[pl...  3.17 us
  transfers between devices with their start and end apart: 1, of which 1 were waited for; matrix products, arithmetic and copies ran while one was open for 0% of the time, Pallas kernels for 6%

profile of v3, /device:TPU:6, one launch (start us, length us, event | category | flops | bytes accessed | tf_op | source)
XLA Modules:
  0.0 145.1 jit_solution(15348900771234721942)
XLA Ops:
  0.0 1.5 %slice.3 = bf16[64,3,1024]{2,1,0:T(4,128)(2,1)S(1)} slice(bf16[64,64,1024]{2,1,0:T(8,128)(2,1)} %samples_ref.3), slice={[0:64], [61:64], [0:1024]} | slice | bytes 786432 | tf_op jit(solution)/shard_map/slice | solution.py:271
  1.5 1.9 %collective-permute-start = (bf16[64,3,1024]{2,1,0:T(4,128)(2,1)S(1)}, bf16[64,3,1024]{2,1,0:T(4,128)(2,1)S(1)}, u32[]{:S(2)}, u32[]{:S(2)}) collective-permute-start(bf16[64,3,1024]{2,1,0:T(4,128)(2,1)S(1)} %slice.3), channel_id=1, source_target_pairs={{0,1},{1,2},{2,3},{3,4},{4,5},{5,6},{6,7},{7,8},{8,9},{9,10},{10,1... | collective-permute-start | bytes 1179656 | tf_op jit(solution)/shard_map/ppermute | solution.py:26
  3.4 0.0 copy-start.2
  3.4 0.7 copy-done.2
  4.2 8.7 %filter_late.1.late_ref = bf16[64,64,1024]{2,1,0:T(8,128)(2,1)S(1)} custom-call(f32[4,1024]{1,0:T(4,128)S(1)} %copy-done.2, bf16[64,64,1024]{2,1,0:T(8,128)(2,1)} %samples_ref.3), custom_call_target="tpu_custom_call" | custom-call | flops 33554432 | bytes 16777216 | tf_op jit(solution)/shard_map/filter_late/pallas_call | solution.py:95
  12.9 0.0 copy-start
  12.9 0.0 copy-start.1
  12.9 2.7 %collective-permute-done.halo_ref = bf16[64,3,1024]{2,1,0:T(4,128)(2,1)S(1)} collective-permute-done((bf16[64,3,1024]{2,1,0:T(4,128)(2,1)S(1)}, bf16[64,3,1024]{2,1,0:T(4,128)(2,1)S(1)}, u32[]{:S(2)}, u32[]{:S(2)}) %collective-permute-start) | collective-permute-done | bytes 393248 | tf_op jit(solution)/shard_map/ppermute | solution.py:26
  15.6 3.2 %filter_early.1 = bf16[64,64,1024]{2,1,0:T(8,128)(2,1)S(1)} custom-call(f32[4,1024]{1,0:T(4,128)S(1)} %copy-done.2, bf16[64,3,1024]{2,1,0:T(4,128)(2,1)S(1)} %collective-permute-done.halo_ref, bf16[64,64,1024]{2,1,0:T(8,128)(2,1)} %samples_ref.3, bf16[64,64,1024]{2,1,0:T(8,128)(2,1)S(1)} %filter_late.1.late_ref), custom_call_target="tpu_custom_call", output_to_operand_aliasing={{}: (3, {})} | custom-call | flops 4194304 | bytes 2097152 | tf_op jit(solution)/shard_map/filter_early/pallas_call | solution.py:118
  18.8 0.0 copy-done
  18.8 0.0 copy-done.1
  18.8 8.2 %channelize.1 = bf16[512,2,32,128]{3,2,1,0:T(8,128)(2,1)} custom-call(bf16[2,512,512]{2,1,0:T(8,128)(2,1)S(1)} %copy-done, f32[2,32,512]{2,1,0:T(8,128)S(1)} %bitcast.8, bf16[2,32,64,1024]{3,2,1,0:T(8,128)(2,1)S(1)} %bitcast.6), custom_call_target="tpu_custom_call" | custom-call | flops 4294967296 | bytes 16777216 | tf_op jit(solution)/shard_map/channelize/pallas_call | solution.py:179
  27.0 108.5 %all_to_all.5 = bf16[128,256,128]{2,1,0:T(8,128)(2,1)S(1)} all-to-all(bf16[128,256,128]{2,1,0:T(8,128)(2,1)} %bitcast.9), channel_id=1, replica_groups=mesh['inp'=8,'tm'=16] {'inp','tm'}, dimensions={0} | all-to-all | bytes 16777216 | tf_op jit(solution)/shard_map/all_to_all | solution.py:280
  135.4 9.6 %correlate.1 = f32[4,2,512,512]{3,2,1,0:T(8,128)} custom-call(bf16[8,16,4,64,128]{4,3,2,1,0:T(8,128)(2,1)S(1)} %bitcast.7), custom_call_target="tpu_custom_call" | custom-call | flops 6442450944 | bytes 16777216 | tf_op jit(solution)/shard_map/correlate/pallas_call | solution.py:244
Async XLA Ops:
  1.5 14.1 %collective-permute-start = (bf16[64,3,1024]{2,1,0:T(4,128)(2,1)S(1)}, bf16[64,3,1024]{2,1,0:T(4,128)(2,1)S(1)}, u32[]{:S(2)}, u32[]{:S(2)}) collective-permute-start(bf16[64,3,1024]{2,1,0:T(4,128)(2,1)S(1)} %slice.3), channel_id=1, source_target_pairs={{0,1},{1,2},{2,3},{3,4},{4,5},{5,6},{6,7},{7,8},{8,9},{9,10},{10,1... | collective-permute-start | bytes 1179656 | tf_op jit(solution)/shard_map/ppermute | solution.py:26
  3.4 0.7 copy-start.2
  12.9 5.9 %copy-start = (bf16[2,512,512]{2,1,0:T(8,128)(2,1)S(1)}, bf16[2,512,512]{2,1,0:T(8,128)(2,1)}, u32[]{:S(2)}) copy-start(bf16[2,512,512]{2,1,0:T(8,128)(2,1)} %constant.5.clone.table_ref) | copy-start | bytes 3145732
  12.9 5.9 %copy-start.1 = (f32[512,64]{0,1:T(8,128)S(1)}, f32[512,64]{0,1:T(8,128)}, u32[]{:S(2)}) copy-start(f32[512,64]{0,1:T(8,128)} %param.5) | copy-start | bytes 393220

commit v4 on v3

--- a/solution.py
+++ b/solution.py
@@ -14,6 +14,7 @@
 LANES = 128
 SUBLANES = 8
 BLOCK = 16
+EARLY_BLOCK = 32
 PAIRS = 8
 SUB = 2
 PITCH = 2 * PAIRS + 1
@@ -55,8 +56,8 @@
     for start in range(0, nfft // 2, LANES):
         near = slice(start, start + LANES)
         far = slice(nfft // 2 + start, nfft // 2 + start + LANES)
-        one = summed_taps(rows_of(near), window_ref, near)[SUBLANES:]
-        two = summed_taps(rows_of(far), window_ref, far)[SUBLANES:]
+        one = summed_taps(rows_of(near), window_ref, near)[SUBLANES:].astype(jnp.bfloat16)
+        two = summed_taps(rows_of(far), window_ref, far)[SUBLANES:].astype(jnp.bfloat16)
         store(near, one + two)
         store(far, one - two)
 
@@ -69,7 +70,7 @@
             return samples_ref[a, :, lanes].astype(jnp.float32)
 
         def store(lanes, rows):
-            out_ref[a, SUBLANES:, lanes] = rows.astype(out_ref.dtype)
+            out_ref[a, SUBLANES:, lanes] = rows
 
         folded(rows_of, window_ref, store, nfft)
 
@@ -85,7 +86,7 @@
             return jnp.concatenate([unused, halo, known], axis=0)
 
         def store(lanes, rows):
-            out_ref[a, :, lanes] = rows.astype(out_ref.dtype)
+            out_ref[a, :, lanes] = rows
 
         folded(rows_of, window_ref, store, nfft)
 
@@ -117,14 +118,14 @@
     inputs, frames, nfft = samples.shape
     return pl.pallas_call(
         filter_early_kernel,
-        grid=(inputs // BLOCK,),
+        grid=(inputs // EARLY_BLOCK,),
         in_specs=[
             pl.BlockSpec(window.shape, lambda i: (0, 0)),
-            pl.BlockSpec((BLOCK, TAPS - 1, nfft), lambda i: (i, 0, 0)),
-            pl.BlockSpec((BLOCK, SUBLANES, nfft), lambda i: (i, 0, 0)),
+            pl.BlockSpec((EARLY_BLOCK, TAPS - 1, nfft), lambda i: (i, 0, 0)),
+            pl.BlockSpec((EARLY_BLOCK, SUBLANES, nfft), lambda i: (i, 0, 0)),
             pl.BlockSpec(memory_space=pl.ANY),
         ],
-        out_specs=pl.BlockSpec((BLOCK, SUBLANES, nfft), lambda i: (i, 0, 0)),
+        out_specs=pl.BlockSpec((EARLY_BLOCK, SUBLANES, nfft), lambda i: (i, 0, 0)),
         out_shape=jax.ShapeDtypeStruct((inputs, frames, nfft), jnp.bfloat16),
         input_output_aliases={3: 0},
         compiler_params=pltpu.CompilerParams(
@@ -140,7 +141,9 @@
 
 
 def channelize_kernel(table_ref, gain_ref, rows_ref, out_ref, turned, gains):
-    _, pairs, frames, nfft = rows_ref.shape
+    _, _, frames, nfft = rows_ref.shape
+    pairs = PAIRS
+    here = pl.program_id(0) * PAIRS
     depth = nfft // 2
     count = table_ref.shape[1] // 2
     lane = lax.broadcasted_iota(jnp.int32, (count, 2 * frames), 1)
@@ -151,7 +154,7 @@
         gain = gains[pl.ds(parity, count, stride=2), :]
         columns = slice(parity * depth, (parity + 1) * depth)
         for s in range(0, pairs, SUB):
-            rows = [rows_ref[h, i, :, columns] for i in range(s, s + SUB) for h in range(2)]
+            rows = [rows_ref[h, here + i, :, columns] for i in range(s, s + SUB) for h in range(2)]
             both = lax.dot_general(
                 table_ref[parity],
                 jnp.concatenate(rows, axis=0),
@@ -182,7 +185,7 @@
         in_specs=[
             pl.BlockSpec(tables.shape, lambda i: (0, 0, 0)),
             pl.BlockSpec((2, PAIRS, channels), lambda i: (0, i, 0)),
-            pl.BlockSpec((2, PAIRS, frames, nfft), lambda i: (0, i, 0, 0)),
+            pl.BlockSpec(memory_space=pltpu.VMEM),
         ],
         out_specs=pl.BlockSpec((channels, 2, PAIRS, 2 * frames), lambda i: (0, 0, i, 0)),
         out_shape=pltpu.HBM((channels, 2, half, 2 * frames), jnp.bfloat16),
@@ -203,6 +206,7 @@
 
 
 def correlate_kernel(frames_all, blocks_ref, out_ref):
+    chan = pl.program_id(0)
     n_time = blocks_ref.shape[1]
     inputs_all = blocks_ref.shape[0] * blocks_ref.shape[3]
     width = blocks_ref.shape[4]
@@ -211,7 +215,7 @@
     first = lax.broadcasted_iota(jnp.int32, (n_inp, pairs, width), 2) < half
     straight, crossed = [], []
     for t in range(n_time):
-        real, imag = blocks_ref[:, t, 0, :pairs], blocks_ref[:, t, 0, pairs:]
+        real, imag = blocks_ref[:, t, chan, :pairs], blocks_ref[:, t, chan, pairs:]
         real_turned = jnp.concatenate([real[..., half:], real[..., :half]], axis=2)
         imag_turned = jnp.concatenate([imag[..., half:], imag[..., :half]], axis=2)
         low_rows = jnp.where(first, real, imag_turned)
@@ -244,7 +248,7 @@
     return pl.pallas_call(
         functools.partial(correlate_kernel, frames_all),
         grid=(chan_dev,),
-        in_specs=[pl.BlockSpec((n_inp, n_time, 1, local, width), lambda i: (0, 0, i, 0, 0))],
+        in_specs=[pl.BlockSpec(memory_space=pltpu.VMEM)],
         out_specs=pl.BlockSpec((1, 2, inputs_all, inputs_all), lambda i: (i, 0, 0, 0)),
         out_shape=jax.ShapeDtypeStruct((chan_dev, 2, inputs_all, inputs_all), jnp.float32),
         compiler_params=pltpu.CompilerParams(
@@ -271,6 +275,7 @@
     tail = samples[:, local_frames - (TAPS - 1) :, :]
     halo = passed_along(tail, "tm", 1)
     window = jnp.asarray(window_table(TAPS, nfft))
+    window = pltpu.with_memory_space_constraint(window, pltpu.HBM)
     tables = jnp.asarray(fourier_tables(channels, nfft))
     samples = pltpu.with_memory_space_constraint(samples, pltpu.HBM)
     late = filter_late(window, samples)

time: 145 us -> 143 us (0.986)
  Pallas kernels: 29.7 us -> 28.2 us
where the time goes in v4:
time: 143 us
  blocking collectives  108 us (76%)
  Pallas kernels  28.2 us (20%)
  waiting for transfers between devices  3.32 us (2%)
  starting transfers between devices  1.92 us (1%)
  local copies, waits for them, and re-layouts  1.51 us (1%)
    all_to_all x1, blocking collectives, on_device(): lax.all_to_all(parcel, ('inp', 'tm'), split_axis=0, concat_axis=0, tiled=...  108 us
    pallas_call x1, Pallas kernels, correlate(): pl.pallas_call(functools.partial(correlate_kernel, frames_all), grid=(cha...  9.04 us
    pallas_call x1, Pallas kernels, filter_late(): pl.pallas_call(filter_late_kernel, grid=(inputs // BLOCK,), in_specs=[pl....  8.83 us
    pallas_call x1, Pallas kernels, channelize(): pl.pallas_call(channelize_kernel, grid=(half // PAIRS,), in_specs=[pl.Blo...  7.62 us
    ppermute x1, waiting for transfers between devices, passed_along(): return lax.ppermute(array, axis, pairs)  3.32 us
  transfers between devices with their start and end apart: 1, of which 1 were waited for; matrix products, arithmetic and copies ran while one was open for 0% of the time, Pallas kernels for 6%

profile of v4, /device:TPU:6, one launch (start us, length us, event | category | flops | bytes accessed | tf_op | source)
XLA Modules:
  0.0 142.8 jit_solution(18371195908093571342)
XLA Ops:
  0.0 1.5 %slice.3 = bf16[64,3,1024]{2,1,0:T(4,128)(2,1)S(1)} slice(bf16[64,64,1024]{2,1,0:T(8,128)(2,1)} %samples_ref.3), slice={[0:64], [61:64], [0:1024]} | slice | bytes 786432 | tf_op jit(solution)/shard_map/slice | solution.py:275
  1.5 1.9 %collective-permute-start = (bf16[64,3,1024]{2,1,0:T(4,128)(2,1)S(1)}, bf16[64,3,1024]{2,1,0:T(4,128)(2,1)S(1)}, u32[]{:S(2)}, u32[]{:S(2)}) collective-permute-start(bf16[64,3,1024]{2,1,0:T(4,128)(2,1)S(1)} %slice.3), channel_id=1, source_target_pairs={{0,1},{1,2},{2,3},{3,4},{4,5},{5,6},{6,7},{7,8},{8,9},{9,10},{10,1... | collective-permute-start | bytes 1179656 | tf_op jit(solution)/shard_map/ppermute | solution.py:27
  3.4 8.8 %filter_late.1.late_ref = bf16[64,64,1024]{2,1,0:T(8,128)(2,1)S(1)} custom-call(f32[4,1024]{1,0:T(4,128)} %constant.4.clone.window_ref, bf16[64,64,1024]{2,1,0:T(8,128)(2,1)} %samples_ref.3), custom_call_target="tpu_custom_call" | custom-call | flops 33554432 | bytes 16777216 | tf_op jit(solution)/shard_map/filter_late/pallas_call | solution.py:96
  12.3 0.0 copy-start
  12.3 0.0 copy-start.1
  12.3 3.3 %collective-permute-done.halo_ref = bf16[64,3,1024]{2,1,0:T(4,128)(2,1)S(1)} collective-permute-done((bf16[64,3,1024]{2,1,0:T(4,128)(2,1)S(1)}, bf16[64,3,1024]{2,1,0:T(4,128)(2,1)S(1)}, u32[]{:S(2)}, u32[]{:S(2)}) %collective-permute-start) | collective-permute-done | bytes 393248 | tf_op jit(solution)/shard_map/ppermute | solution.py:27
  15.6 2.7 %filter_early.1 = bf16[64,64,1024]{2,1,0:T(8,128)(2,1)S(1)} custom-call(f32[4,1024]{1,0:T(4,128)} %constant.4.clone.window_ref, bf16[64,3,1024]{2,1,0:T(4,128)(2,1)S(1)} %collective-permute-done.halo_ref, bf16[64,64,1024]{2,1,0:T(8,128)(2,1)} %samples_ref.3, bf16[64,64,1024]{2,1,0:T(8,128)(2,1)S(1)} %filter_late.1.late_ref), custom_call_target="tpu_custom_call", output_to_operand_aliasing={{}: (3, {})} | custom-call | flops 4194304 | bytes 2097152 | tf_op jit(solution)/shard_map/filter_early/pallas_call | solution.py:119
  18.3 0.0 copy-done
  18.3 0.0 copy-done.1
  18.3 7.6 %channelize.1 = bf16[512,2,32,128]{3,2,1,0:T(8,128)(2,1)} custom-call(bf16[2,512,512]{2,1,0:T(8,128)(2,1)S(1)} %copy-done, f32[2,32,512]{2,1,0:T(8,128)S(1)} %bitcast.8, bf16[2,32,64,1024]{3,2,1,0:T(8,128)(2,1)S(1)} %bitcast.6), custom_call_target="tpu_custom_call" | custom-call | flops 4294967296 | bytes 16777216 | tf_op jit(solution)/shard_map/channelize/pallas_call | solution.py:182
  26.0 107.8 %all_to_all.5 = bf16[128,256,128]{2,1,0:T(8,128)(2,1)S(1)} all-to-all(bf16[128,256,128]{2,1,0:T(8,128)(2,1)} %bitcast.9), channel_id=1, replica_groups=mesh['inp'=8,'tm'=16] {'inp','tm'}, dimensions={0} | all-to-all | bytes 16777216 | tf_op jit(solution)/shard_map/all_to_all | solution.py:285
  133.8 9.0 %correlate.1 = f32[4,2,512,512]{3,2,1,0:T(8,128)} custom-call(bf16[8,16,4,64,128]{4,3,2,1,0:T(8,128)(2,1)S(1)} %bitcast.7), custom_call_target="tpu_custom_call" | custom-call | flops 6442450944 | bytes 16777216 | tf_op jit(solution)/shard_map/correlate/pallas_call | solution.py:248
Async XLA Ops:
  1.5 14.1 %collective-permute-start = (bf16[64,3,1024]{2,1,0:T(4,128)(2,1)S(1)}, bf16[64,3,1024]{2,1,0:T(4,128)(2,1)S(1)}, u32[]{:S(2)}, u32[]{:S(2)}) collective-permute-start(bf16[64,3,1024]{2,1,0:T(4,128)(2,1)S(1)} %slice.3), channel_id=1, source_target_pairs={{0,1},{1,2},{2,3},{3,4},{4,5},{5,6},{6,7},{7,8},{8,9},{9,10},{10,1... | collective-permute-start | bytes 1179656 | tf_op jit(solution)/shard_map/ppermute | solution.py:27
  12.3 6.0 %copy-start = (bf16[2,512,512]{2,1,0:T(8,128)(2,1)S(1)}, bf16[2,512,512]{2,1,0:T(8,128)(2,1)}, u32[]{:S(2)}) copy-start(bf16[2,512,512]{2,1,0:T(8,128)(2,1)} %constant.5.clone.table_ref) | copy-start | bytes 3145732
  12.3 6.0 %copy-start.1 = (f32[512,64]{0,1:T(8,128)S(1)}, f32[512,64]{0,1:T(8,128)}, u32[]{:S(2)}) copy-start(f32[512,64]{0,1:T(8,128)} %param.5) | copy-start | bytes 393220

commit v5 on v4

--- a/solution.py
+++ b/solution.py
@@ -45,50 +45,50 @@
     return table.reshape(2, channels, nfft // 2)
 
 
-def summed_taps(frames, window_ref, lanes):
-    window = [window_ref[tap : tap + 1, lanes] for tap in range(TAPS)]
+def summed_taps(frames, window):
     earlier = pltpu.roll(frames, 2, 0)
     odd = frames * window[2] + earlier * window[0]
     return frames * window[3] + earlier * window[1] + pltpu.roll(odd, 1, 0)
 
 
-def folded(rows_of, window_ref, store, nfft):
+def folded(rows_of, window_ref, store, inputs, nfft):
     for start in range(0, nfft // 2, LANES):
-        near = slice(start, start + LANES)
-        far = slice(nfft // 2 + start, nfft // 2 + start + LANES)
-        one = summed_taps(rows_of(near), window_ref, near)[SUBLANES:].astype(jnp.bfloat16)
-        two = summed_taps(rows_of(far), window_ref, far)[SUBLANES:].astype(jnp.bfloat16)
-        store(near, one + two)
-        store(far, one - two)
+        halves = [slice(at, at + LANES) for at in (start, nfft // 2 + start)]
+        windows = [[window_ref[tap : tap + 1, h] for tap in range(TAPS)] for h in halves]
+        for a in range(inputs):
+            near, far = [
+                summed_taps(rows_of(a, h), window)[SUBLANES:].astype(jnp.bfloat16)
+                for h, window in zip(halves, windows)
+            ]
+            store(a, halves[0], near + far)
+            store(a, halves[1], near - far)
 
 
 def filter_late_kernel(window_ref, samples_ref, out_ref):
     inputs, frames, nfft = samples_ref.shape
-    for a in range(inputs):
-
-        def rows_of(lanes):
-            return samples_ref[a, :, lanes].astype(jnp.float32)
-
-        def store(lanes, rows):
-            out_ref[a, SUBLANES:, lanes] = rows
-
-        folded(rows_of, window_ref, store, nfft)
+
+    def rows_of(a, lanes):
+        return samples_ref[a, :, lanes].astype(jnp.float32)
+
+    def store(a, lanes, rows):
+        out_ref[a, SUBLANES:, lanes] = rows
+
+    folded(rows_of, window_ref, store, inputs, nfft)
 
 
 def filter_early_kernel(window_ref, halo_ref, samples_ref, late_ref, out_ref):
     inputs, frames, nfft = samples_ref.shape
     unused = jnp.zeros((SUBLANES - (TAPS - 1), LANES), jnp.float32)
-    for a in range(inputs):
-
-        def rows_of(lanes):
-            halo = halo_ref[a, :, lanes].astype(jnp.float32)
-            known = samples_ref[a, :, lanes].astype(jnp.float32)
-            return jnp.concatenate([unused, halo, known], axis=0)
-
-        def store(lanes, rows):
-            out_ref[a, :, lanes] = rows
-
-        folded(rows_of, window_ref, store, nfft)
+
+    def rows_of(a, lanes):
+        halo = halo_ref[a, :, lanes].astype(jnp.float32)
+        known = samples_ref[a, :, lanes].astype(jnp.float32)
+        return jnp.concatenate([unused, halo, known], axis=0)
+
+    def store(a, lanes, rows):
+        out_ref[a, :, lanes] = rows
+
+    folded(rows_of, window_ref, store, inputs, nfft)
 
 
 def filter_late(window, samples):
@@ -207,39 +207,36 @@
 
 def correlate_kernel(frames_all, blocks_ref, out_ref):
     chan = pl.program_id(0)
-    n_time = blocks_ref.shape[1]
-    inputs_all = blocks_ref.shape[0] * blocks_ref.shape[3]
-    width = blocks_ref.shape[4]
-    half = width // 2
-    n_inp, pairs = blocks_ref.shape[0], blocks_ref.shape[3] // 2
+    n_inp, n_time, _, local, width = blocks_ref.shape
+    pairs, half = local // 2, width // 2
+    inputs_all = n_inp * local
     first = lax.broadcasted_iota(jnp.int32, (n_inp, pairs, width), 2) < half
-    straight, crossed = [], []
-    for t in range(n_time):
-        real, imag = blocks_ref[:, t, chan, :pairs], blocks_ref[:, t, chan, pairs:]
-        real_turned = jnp.concatenate([real[..., half:], real[..., :half]], axis=2)
-        imag_turned = jnp.concatenate([imag[..., half:], imag[..., :half]], axis=2)
-        low_rows = jnp.where(first, real, imag_turned)
-        high_rows = jnp.where(first, real_turned, imag)
-        rows = jnp.concatenate([low_rows, high_rows], axis=1)
-        straight.append(rows.reshape(inputs_all, width))
-        low_rows = jnp.where(first, imag, -real_turned)
-        high_rows = jnp.where(first, imag_turned, -real)
-        rows = jnp.concatenate([low_rows, high_rows], axis=1)
-        crossed.append(rows.reshape(inputs_all, width))
-    straight = jnp.concatenate(straight, axis=1)
-    crossed = jnp.concatenate(crossed, axis=1)
+    parts = []
+    for rows in (slice(0, pairs), slice(pairs, local)):
+        columns = []
+        for t in range(0, n_time, 2):
+            one, two = blocks_ref[:, t, chan, rows], blocks_ref[:, t + 1, chan, rows]
+            one_turned = jnp.concatenate([one[..., half:], one[..., :half]], axis=2)
+            two_turned = jnp.concatenate([two[..., half:], two[..., :half]], axis=2)
+            low_rows = jnp.where(first, one, two_turned)
+            high_rows = jnp.where(first, one_turned, two)
+            both = jnp.concatenate([low_rows, high_rows], axis=1)
+            columns.append(both.reshape(inputs_all, width))
+        parts.append(jnp.concatenate(columns, axis=1))
+    real, imag = parts
+    spectra = jnp.concatenate(parts, axis=1)
     last = (((1,), (1,)), ((), ()))
     scale = 1.0 / frames_all
     low, high = slice(0, inputs_all // 2), slice(inputs_all // 2, inputs_all)
     for rows, columns in ((low, low), (high, low), (high, high)):
-        for k, left in enumerate((straight, crossed)):
-            product = scale * lax.dot_general(
-                left[rows], straight[columns], last, preferred_element_type=jnp.float32
-            )
-            out_ref[0, k, rows, columns] = product
-            if rows != columns:
-                mirrored = product.T
-                out_ref[0, k, columns, rows] = mirrored if k == 0 else -mirrored
+        product = scale * lax.dot_general(
+            spectra[rows], spectra[columns], last, preferred_element_type=jnp.float32
+        )
+        out_ref[0, 0, rows, columns] = product
+        if rows != columns:
+            out_ref[0, 0, columns, rows] = product.T
+    product = scale * lax.dot_general(imag, real, last, preferred_element_type=jnp.float32)
+    out_ref[0, 1] = product - product.T
 
 
 def correlate(arrived, frames_all):

time: 143 us -> 142 us (level)
  no operation moved by 1% of the time
where the time goes in v5:
time: 142 us
  blocking collectives  108 us (76%)
  Pallas kernels  27.4 us (19%)
  waiting for transfers between devices  3.32 us (2%)
  starting transfers between devices  1.92 us (1%)
  local copies, waits for them, and re-layouts  1.51 us (1%)
    all_to_all x1, blocking collectives, on_device(): lax.all_to_all(parcel, ('inp', 'tm'), split_axis=0, concat_axis=0, tiled=...  108 us
    pallas_call x1, Pallas kernels, filter_late(): pl.pallas_call(filter_late_kernel, grid=(inputs // BLOCK,), in_specs=[pl....  8.83 us
    pallas_call x1, Pallas kernels, correlate(): pl.pallas_call(functools.partial(correlate_kernel, frames_all), grid=(cha...  8.23 us
    pallas_call x1, Pallas kernels, channelize(): pl.pallas_call(channelize_kernel, grid=(half // PAIRS,), in_specs=[pl.Blo...  7.62 us
    ppermute x1, waiting for transfers between devices, passed_along(): return lax.ppermute(array, axis, pairs)  3.32 us
  transfers between devices with their start and end apart: 1, of which 1 were waited for; matrix products, arithmetic and copies ran while one was open for 0% of the time, Pallas kernels for 6%

profile of v5, /device:TPU:6, one launch (start us, length us, event | category | flops | bytes accessed | tf_op | source)
XLA Modules:
  0.0 142.0 jit_solution(8306837595681741183)
XLA Ops:
  0.0 1.5 %slice.3 = bf16[64,3,1024]{2,1,0:T(4,128)(2,1)S(1)} slice(bf16[64,64,1024]{2,1,0:T(8,128)(2,1)} %samples_ref.3), slice={[0:64], [61:64], [0:1024]} | slice | bytes 786432 | tf_op jit(solution)/shard_map/slice | solution.py:272
  1.5 1.9 %collective-permute-start = (bf16[64,3,1024]{2,1,0:T(4,128)(2,1)S(1)}, bf16[64,3,1024]{2,1,0:T(4,128)(2,1)S(1)}, u32[]{:S(2)}, u32[]{:S(2)}) collective-permute-start(bf16[64,3,1024]{2,1,0:T(4,128)(2,1)S(1)} %slice.3), channel_id=1, source_target_pairs={{0,1},{1,2},{2,3},{3,4},{4,5},{5,6},{6,7},{7,8},{8,9},{9,10},{10,1... | collective-permute-start | bytes 1179656 | tf_op jit(solution)/shard_map/ppermute | solution.py:27
  3.4 8.8 %filter_late.1.late_ref = bf16[64,64,1024]{2,1,0:T(8,128)(2,1)S(1)} custom-call(f32[4,1024]{1,0:T(4,128)} %constant.4.clone.window_ref, bf16[64,64,1024]{2,1,0:T(8,128)(2,1)} %samples_ref.3), custom_call_target="tpu_custom_call" | custom-call | flops 33554432 | bytes 16777216 | tf_op jit(solution)/shard_map/filter_late/pallas_call | solution.py:96
  12.3 0.0 copy-start
  12.3 0.0 copy-start.1
  12.3 3.3 %collective-permute-done.halo_ref = bf16[64,3,1024]{2,1,0:T(4,128)(2,1)S(1)} collective-permute-done((bf16[64,3,1024]{2,1,0:T(4,128)(2,1)S(1)}, bf16[64,3,1024]{2,1,0:T(4,128)(2,1)S(1)}, u32[]{:S(2)}, u32[]{:S(2)}) %collective-permute-start) | collective-permute-done | bytes 393248 | tf_op jit(solution)/shard_map/ppermute | solution.py:27
  15.6 2.7 %filter_early.1 = bf16[64,64,1024]{2,1,0:T(8,128)(2,1)S(1)} custom-call(f32[4,1024]{1,0:T(4,128)} %constant.4.clone.window_ref, bf16[64,3,1024]{2,1,0:T(4,128)(2,1)S(1)} %collective-permute-done.halo_ref, bf16[64,64,1024]{2,1,0:T(8,128)(2,1)} %samples_ref.3, bf16[64,64,1024]{2,1,0:T(8,128)(2,1)S(1)} %filter_late.1.late_ref), custom_call_target="tpu_custom_call", output_to_operand_aliasing={{}: (3, {})} | custom-call | flops 4194304 | bytes 2097152 | tf_op jit(solution)/shard_map/filter_early/pallas_call | solution.py:119
  18.3 0.0 copy-done
  18.3 0.0 copy-done.1
  18.3 7.6 %channelize.1 = bf16[512,2,32,128]{3,2,1,0:T(8,128)(2,1)} custom-call(bf16[2,512,512]{2,1,0:T(8,128)(2,1)S(1)} %copy-done, f32[2,32,512]{2,1,0:T(8,128)S(1)} %bitcast.8, bf16[2,32,64,1024]{3,2,1,0:T(8,128)(2,1)S(1)} %bitcast.6), custom_call_target="tpu_custom_call" | custom-call | flops 4294967296 | bytes 16777216 | tf_op jit(solution)/shard_map/channelize/pallas_call | solution.py:182
  26.0 107.8 %all_to_all.5 = bf16[128,256,128]{2,1,0:T(8,128)(2,1)S(1)} all-to-all(bf16[128,256,128]{2,1,0:T(8,128)(2,1)} %bitcast.9), channel_id=1, replica_groups=mesh['inp'=8,'tm'=16] {'inp','tm'}, dimensions={0} | all-to-all | bytes 16777216 | tf_op jit(solution)/shard_map/all_to_all | solution.py:282
  133.8 8.2 %correlate.1 = f32[4,2,512,512]{3,2,1,0:T(8,128)} custom-call(bf16[8,16,4,64,128]{4,3,2,1,0:T(8,128)(2,1)S(1)} %bitcast.7), custom_call_target="tpu_custom_call" | custom-call | flops 6442450944 | bytes 16777216 | tf_op jit(solution)/shard_map/correlate/pallas_call | solution.py:245
Async XLA Ops:
  1.5 14.1 %collective-permute-start = (bf16[64,3,1024]{2,1,0:T(4,128)(2,1)S(1)}, bf16[64,3,1024]{2,1,0:T(4,128)(2,1)S(1)}, u32[]{:S(2)}, u32[]{:S(2)}) collective-permute-start(bf16[64,3,1024]{2,1,0:T(4,128)(2,1)S(1)} %slice.3), channel_id=1, source_target_pairs={{0,1},{1,2},{2,3},{3,4},{4,5},{5,6},{6,7},{7,8},{8,9},{9,10},{10,1... | collective-permute-start | bytes 1179656 | tf_op jit(solution)/shard_map/ppermute | solution.py:27
  12.3 6.1 %copy-start = (bf16[2,512,512]{2,1,0:T(8,128)(2,1)S(1)}, bf16[2,512,512]{2,1,0:T(8,128)(2,1)}, u32[]{:S(2)}) copy-start(bf16[2,512,512]{2,1,0:T(8,128)(2,1)} %constant.5.clone.table_ref) | copy-start | bytes 3145732
  12.3 6.0 %copy-start.1 = (f32[512,64]{0,1:T(8,128)S(1)}, f32[512,64]{0,1:T(8,128)}, u32[]{:S(2)}) copy-start(f32[512,64]{0,1:T(8,128)} %param.5) | copy-start | bytes 393220

commit v6 on v5

--- a/solution.py
+++ b/solution.py
@@ -188,7 +188,7 @@
             pl.BlockSpec(memory_space=pltpu.VMEM),
         ],
         out_specs=pl.BlockSpec((channels, 2, PAIRS, 2 * frames), lambda i: (0, 0, i, 0)),
-        out_shape=pltpu.HBM((channels, 2, half, 2 * frames), jnp.bfloat16),
+        out_shape=jax.ShapeDtypeStruct((channels, 2, half, 2 * frames), jnp.bfloat16),
         scratch_shapes=[
             pltpu.VMEM((channels * PITCH, 2 * frames), jnp.float32),
             pltpu.VMEM((channels, LANES), jnp.float32),

time: 142 us -> 142 us (level)
  no operation moved by 1% of the time
where the time goes in v6:
time: 142 us
  blocking collectives  108 us (76%)
  Pallas kernels  27.5 us (19%)
  waiting for transfers between devices  3.32 us (2%)
  starting transfers between devices  1.92 us (1%)
  local copies, waits for them, and re-layouts  1.51 us (1%)
    all_to_all x1, blocking collectives, on_device(): lax.all_to_all(parcel, ('inp', 'tm'), split_axis=0, concat_axis=0, tiled=...  108 us
    pallas_call x1, Pallas kernels, filter_late(): pl.pallas_call(filter_late_kernel, grid=(inputs // BLOCK,), in_specs=[pl....  8.83 us
    pallas_call x1, Pallas kernels, correlate(): pl.pallas_call(functools.partial(correlate_kernel, frames_all), grid=(cha...  8.23 us
    pallas_call x1, Pallas kernels, channelize(): pl.pallas_call(channelize_kernel, grid=(half // PAIRS,), in_specs=[pl.Blo...  7.74 us
    ppermute x1, waiting for transfers between devices, passed_along(): return lax.ppermute(array, axis, pairs)  3.32 us
  transfers between devices with their start and end apart: 1, of which 1 were waited for; matrix products, arithmetic and copies ran while one was open for 0% of the time, Pallas kernels for 6%

profile of v6, /device:TPU:6, one launch (start us, length us, event | category | flops | bytes accessed | tf_op | source)
XLA Modules:
  0.0 142.0 jit_solution(16570230470137282792)
XLA Ops:
  0.0 1.5 %slice.3 = bf16[64,3,1024]{2,1,0:T(4,128)(2,1)S(1)} slice(bf16[64,64,1024]{2,1,0:T(8,128)(2,1)} %samples_ref.3), slice={[0:64], [61:64], [0:1024]} | slice | bytes 786432 | tf_op jit(solution)/shard_map/slice | solution.py:272
  1.5 1.9 %collective-permute-start = (bf16[64,3,1024]{2,1,0:T(4,128)(2,1)S(1)}, bf16[64,3,1024]{2,1,0:T(4,128)(2,1)S(1)}, u32[]{:S(2)}, u32[]{:S(2)}) collective-permute-start(bf16[64,3,1024]{2,1,0:T(4,128)(2,1)S(1)} %slice.3), channel_id=1, source_target_pairs={{0,1},{1,2},{2,3},{3,4},{4,5},{5,6},{6,7},{7,8},{8,9},{9,10},{10,1... | collective-permute-start | bytes 1179656 | tf_op jit(solution)/shard_map/ppermute | solution.py:27
  3.4 8.8 %filter_late.1.late_ref = bf16[64,64,1024]{2,1,0:T(8,128)(2,1)S(1)} custom-call(f32[4,1024]{1,0:T(4,128)} %constant.4.clone.window_ref, bf16[64,64,1024]{2,1,0:T(8,128)(2,1)} %samples_ref.3), custom_call_target="tpu_custom_call" | custom-call | flops 33554432 | bytes 16777216 | tf_op jit(solution)/shard_map/filter_late/pallas_call | solution.py:96
  12.3 0.0 copy-start
  12.3 0.0 copy-start.1
  12.3 3.3 %collective-permute-done.halo_ref = bf16[64,3,1024]{2,1,0:T(4,128)(2,1)S(1)} collective-permute-done((bf16[64,3,1024]{2,1,0:T(4,128)(2,1)S(1)}, bf16[64,3,1024]{2,1,0:T(4,128)(2,1)S(1)}, u32[]{:S(2)}, u32[]{:S(2)}) %collective-permute-start) | collective-permute-done | bytes 393248 | tf_op jit(solution)/shard_map/ppermute | solution.py:27
  15.6 2.7 %filter_early.1 = bf16[64,64,1024]{2,1,0:T(8,128)(2,1)S(1)} custom-call(f32[4,1024]{1,0:T(4,128)} %constant.4.clone.window_ref, bf16[64,3,1024]{2,1,0:T(4,128)(2,1)S(1)} %collective-permute-done.halo_ref, bf16[64,64,1024]{2,1,0:T(8,128)(2,1)} %samples_ref.3, bf16[64,64,1024]{2,1,0:T(8,128)(2,1)S(1)} %filter_late.1.late_ref), custom_call_target="tpu_custom_call", output_to_operand_aliasing={{}: (3, {})} | custom-call | flops 4194304 | bytes 2097152 | tf_op jit(solution)/shard_map/filter_early/pallas_call | solution.py:119
  18.3 0.0 copy-done
  18.3 0.0 copy-done.1
  18.3 7.7 %channelize.1 = bf16[512,2,32,128]{3,2,1,0:T(8,128)(2,1)S(1)} custom-call(bf16[2,512,512]{2,1,0:T(8,128)(2,1)S(1)} %copy-done, f32[2,32,512]{2,1,0:T(8,128)S(1)} %bitcast.9, bf16[2,32,64,1024]{3,2,1,0:T(8,128)(2,1)S(1)} %bitcast.6), custom_call_target="tpu_custom_call" | custom-call | flops 4294967296 | bytes 16777216 | tf_op jit(solution)/shard_map/channelize/pallas_call | solution.py:182
  26.1 107.6 %all_to_all.5 = bf16[128,256,128]{2,1,0:T(8,128)(2,1)S(1)} all-to-all(bf16[128,256,128]{2,1,0:T(8,128)(2,1)S(1)} %bitcast.7), channel_id=1, replica_groups=mesh['inp'=8,'tm'=16] {'inp','tm'}, dimensions={0} | all-to-all | bytes 16777216 | tf_op jit(solution)/shard_map/all_to_all | solution.py:282
  133.7 8.2 %correlate.1 = f32[4,2,512,512]{3,2,1,0:T(8,128)} custom-call(bf16[8,16,4,64,128]{4,3,2,1,0:T(8,128)(2,1)S(1)} %bitcast.8), custom_call_target="tpu_custom_call" | custom-call | flops 6442450944 | bytes 16777216 | tf_op jit(solution)/shard_map/correlate/pallas_call | solution.py:245
Async XLA Ops:
  1.5 14.1 %collective-permute-start = (bf16[64,3,1024]{2,1,0:T(4,128)(2,1)S(1)}, bf16[64,3,1024]{2,1,0:T(4,128)(2,1)S(1)}, u32[]{:S(2)}, u32[]{:S(2)}) collective-permute-start(bf16[64,3,1024]{2,1,0:T(4,128)(2,1)S(1)} %slice.3), channel_id=1, source_target_pairs={{0,1},{1,2},{2,3},{3,4},{4,5},{5,6},{6,7},{7,8},{8,9},{9,10},{10,1... | collective-permute-start | bytes 1179656 | tf_op jit(solution)/shard_map/ppermute | solution.py:27
  12.3 6.1 %copy-start = (bf16[2,512,512]{2,1,0:T(8,128)(2,1)S(1)}, bf16[2,512,512]{2,1,0:T(8,128)(2,1)}, u32[]{:S(2)}) copy-start(bf16[2,512,512]{2,1,0:T(8,128)(2,1)} %constant.5.clone.table_ref) | copy-start | bytes 3145732
  12.3 6.0 %copy-start.1 = (f32[512,64]{0,1:T(8,128)S(1)}, f32[512,64]{0,1:T(8,128)}, u32[]{:S(2)}) copy-start(f32[512,64]{0,1:T(8,128)} %param.5) | copy-start | bytes 393220

commit v7 on v5

--- a/solution.py
+++ b/solution.py
@@ -51,113 +51,45 @@
     return frames * window[3] + earlier * window[1] + pltpu.roll(odd, 1, 0)
 
 
-def folded(rows_of, window_ref, store, inputs, nfft):
+def folded(halo, samples, window_ref):
+    nfft = samples.shape[1]
+    unused = jnp.zeros((SUBLANES - (TAPS - 1), LANES), jnp.float32)
+    sums, differences = [], []
     for start in range(0, nfft // 2, LANES):
-        halves = [slice(at, at + LANES) for at in (start, nfft // 2 + start)]
-        windows = [[window_ref[tap : tap + 1, h] for tap in range(TAPS)] for h in halves]
-        for a in range(inputs):
-            near, far = [
-                summed_taps(rows_of(a, h), window)[SUBLANES:].astype(jnp.bfloat16)
-                for h, window in zip(halves, windows)
-            ]
-            store(a, halves[0], near + far)
-            store(a, halves[1], near - far)
-
-
-def filter_late_kernel(window_ref, samples_ref, out_ref):
-    inputs, frames, nfft = samples_ref.shape
-
-    def rows_of(a, lanes):
-        return samples_ref[a, :, lanes].astype(jnp.float32)
-
-    def store(a, lanes, rows):
-        out_ref[a, SUBLANES:, lanes] = rows
-
-    folded(rows_of, window_ref, store, inputs, nfft)
-
-
-def filter_early_kernel(window_ref, halo_ref, samples_ref, late_ref, out_ref):
-    inputs, frames, nfft = samples_ref.shape
-    unused = jnp.zeros((SUBLANES - (TAPS - 1), LANES), jnp.float32)
-
-    def rows_of(a, lanes):
-        halo = halo_ref[a, :, lanes].astype(jnp.float32)
-        known = samples_ref[a, :, lanes].astype(jnp.float32)
-        return jnp.concatenate([unused, halo, known], axis=0)
-
-    def store(a, lanes, rows):
-        out_ref[a, :, lanes] = rows
-
-    folded(rows_of, window_ref, store, inputs, nfft)
-
-
-def filter_late(window, samples):
-    inputs, frames, nfft = samples.shape
-    return pl.pallas_call(
-        filter_late_kernel,
-        grid=(inputs // BLOCK,),
-        in_specs=[
-            pl.BlockSpec(window.shape, lambda i: (0, 0)),
-            pl.BlockSpec((BLOCK, frames, nfft), lambda i: (i, 0, 0)),
-        ],
-        out_specs=pl.BlockSpec((BLOCK, frames, nfft), lambda i: (i, 0, 0)),
-        out_shape=jax.ShapeDtypeStruct((inputs, frames, nfft), jnp.bfloat16),
-        compiler_params=pltpu.CompilerParams(
-            dimension_semantics=("arbitrary",), vmem_limit_bytes=16 * MIB
-        ),
-        cost_estimate=pl.CostEstimate(
-            flops=2 * TAPS * inputs * frames * nfft,
-            transcendentals=0,
-            bytes_accessed=4 * inputs * frames * nfft,
-        ),
-        name="filter_late",
-    )(window, samples)
-
-
-def filter_early(window, halo, samples, late):
-    inputs, frames, nfft = samples.shape
-    return pl.pallas_call(
-        filter_early_kernel,
-        grid=(inputs // EARLY_BLOCK,),
-        in_specs=[
-            pl.BlockSpec(window.shape, lambda i: (0, 0)),
-            pl.BlockSpec((EARLY_BLOCK, TAPS - 1, nfft), lambda i: (i, 0, 0)),
-            pl.BlockSpec((EARLY_BLOCK, SUBLANES, nfft), lambda i: (i, 0, 0)),
-            pl.BlockSpec(memory_space=pl.ANY),
-        ],
-        out_specs=pl.BlockSpec((EARLY_BLOCK, SUBLANES, nfft), lambda i: (i, 0, 0)),
-        out_shape=jax.ShapeDtypeStruct((inputs, frames, nfft), jnp.bfloat16),
-        input_output_aliases={3: 0},
-        compiler_params=pltpu.CompilerParams(
-            dimension_semantics=("arbitrary",), vmem_limit_bytes=16 * MIB
-        ),
-        cost_estimate=pl.CostEstimate(
-            flops=2 * TAPS * inputs * SUBLANES * nfft,
-            transcendentals=0,
-            bytes_accessed=4 * inputs * SUBLANES * nfft,
-        ),
-        name="filter_early",
-    )(window, halo, samples, late)
-
-
-def channelize_kernel(table_ref, gain_ref, rows_ref, out_ref, turned, gains):
-    _, _, frames, nfft = rows_ref.shape
-    pairs = PAIRS
-    here = pl.program_id(0) * PAIRS
-    depth = nfft // 2
+        parts = []
+        for at in (start, nfft // 2 + start):
+            lanes = slice(at, at + LANES)
+            window = [window_ref[tap : tap + 1, lanes] for tap in range(TAPS)]
+            known = [unused, halo[:, lanes].astype(jnp.float32)]
+            known.append(samples[:, lanes].astype(jnp.float32))
+            total = summed_taps(jnp.concatenate(known, axis=0), window)
+            parts.append(total[SUBLANES:].astype(jnp.bfloat16))
+        sums.append(parts[0] + parts[1])
+        differences.append(parts[0] - parts[1])
+    return jnp.concatenate(sums, axis=1), jnp.concatenate(differences, axis=1)
+
+
+def channelize_kernel(
+    table_ref, gain_ref, window_ref, halo_ref, samples_ref, out_ref, turned, gains
+):
+    _, pairs, frames, _ = samples_ref.shape
     count = table_ref.shape[1] // 2
     lane = lax.broadcasted_iota(jnp.int32, (count, 2 * frames), 1)
     first = lane < frames
     unused = jnp.zeros((LANES - 2 * pairs, 2 * count), jnp.float32)
     gains[...] = jnp.transpose(jnp.concatenate([gain_ref[0], gain_ref[1], unused], axis=0))
-    for parity in range(2):
-        gain = gains[pl.ds(parity, count, stride=2), :]
-        columns = slice(parity * depth, (parity + 1) * depth)
-        for s in range(0, pairs, SUB):
-            rows = [rows_ref[h, here + i, :, columns] for i in range(s, s + SUB) for h in range(2)]
+    gain_of = [gains[pl.ds(parity, count, stride=2), :] for parity in range(2)]
+    for s in range(0, pairs, SUB):
+        filtered = [
+            folded(halo_ref[h, i], samples_ref[h, i], window_ref)
+            for i in range(s, s + SUB)
+            for h in range(2)
+        ]
+        for parity in range(2):
+            gain = gain_of[parity]
             both = lax.dot_general(
                 table_ref[parity],
-                jnp.concatenate(rows, axis=0),
+                jnp.concatenate([rows[parity] for rows in filtered], axis=0),
                 (((1,), (1,)), ((), ())),
                 preferred_element_type=jnp.float32,
             )
@@ -175,8 +107,8 @@
                 out_ref[2 * c + parity, r] = rows.astype(out_ref.dtype)
 
 
-def channelize(tables, gain, rows):
-    inputs, frames, nfft = rows.shape
+def channelize(tables, gain, window, halo, samples):
+    inputs, frames, nfft = samples.shape
     channels = tables.shape[1]
     half = inputs // 2
     return pl.pallas_call(
@@ -185,7 +117,9 @@
         in_specs=[
             pl.BlockSpec(tables.shape, lambda i: (0, 0, 0)),
             pl.BlockSpec((2, PAIRS, channels), lambda i: (0, i, 0)),
-            pl.BlockSpec(memory_space=pltpu.VMEM),
+            pl.BlockSpec(window.shape, lambda i: (0, 0)),
+            pl.BlockSpec((2, PAIRS, TAPS - 1, nfft), lambda i: (0, i, 0, 0)),
+            pl.BlockSpec((2, PAIRS, frames, nfft), lambda i: (0, i, 0, 0)),
         ],
         out_specs=pl.BlockSpec((channels, 2, PAIRS, 2 * frames), lambda i: (0, 0, i, 0)),
         out_shape=pltpu.HBM((channels, 2, half, 2 * frames), jnp.bfloat16),
@@ -202,7 +136,15 @@
             bytes_accessed=2 * (inputs * frames * nfft + channels * inputs * 2 * frames),
         ),
         name="channelize",
-    )(tables, gain.reshape(2, half, channels), rows.reshape(2, half, frames, nfft))
+    )(
+        tables,
+        gain.reshape(2, half, channels),
+        window,
+        halo.reshape(2, half, TAPS - 1, nfft),
+        pltpu.with_memory_space_constraint(
+            samples.reshape(2, half, frames, nfft), pltpu.HBM
+        ),
+    )
 
 
 def correlate_kernel(frames_all, blocks_ref, out_ref):
@@ -274,10 +216,7 @@
     window = jnp.asarray(window_table(TAPS, nfft))
     window = pltpu.with_memory_space_constraint(window, pltpu.HBM)
     tables = jnp.asarray(fourier_tables(channels, nfft))
-    samples = pltpu.with_memory_space_constraint(samples, pltpu.HBM)
-    late = filter_late(window, samples)
-    rows = filter_early(window, halo, samples, late)
-    parcel = channelize(tables, eq_gain.T, rows)
+    parcel = channelize(tables, eq_gain.T, window, halo, samples)
     parcel = parcel.reshape(groups, chan_dev * local_inputs, 2 * local_frames)
     arrived = lax.all_to_all(parcel, ("inp", "tm"), split_axis=0, concat_axis=0, tiled=True)
     arrived = arrived.reshape(n_inp, n_time, chan_dev, local_inputs, 2 * local_frames)

time: 142 us -> 148 us (1.042)
  waiting for transfers between devices: 3.32 us -> 10.8 us
  Pallas kernels: 27.4 us -> 23.1 us
  local copies, waits for them, and re-layouts: 1.51 us -> 4.12 us
    pallas_call x2 -> x0, Pallas kernels: 11.5 us -> none  [the longest x1 8.83 us: filter_late(): pl.pallas_call(filter_late_kernel, grid=(inputs // BLOCK,), in_specs=[pl....]
    ppermute x1, waiting for transfers between devices: 3.32 us -> 10.8 us  [passed_along(): return lax.ppermute(array, axis, pairs)]
    pallas_call x1, Pallas kernels: 7.62 us -> 14.9 us  [channelize(): pl.pallas_call(channelize_kernel, grid=(half // PAIRS,), in_specs=[pl.Blo...]
    unnamed x4 -> x5, local copies, waits for them, and re-layouts: 0.01 us -> 2.28 us
  transfers between devices with their start and end apart: 1 -> 1, of which waited for: 1 -> 1; matrix products, arithmetic and copies ran while one was open for 0% -> 0% of each run, Pallas kernels for 6% -> 0%
where the time goes in v7:
time: 148 us; the launch traced here: 147 us
  blocking collectives  107 us (72%)
  Pallas kernels  23.1 us (16%)
  waiting for transfers between devices  10.8 us (7%)
  local copies, waits for them, and re-layouts  4.12 us (3%)
  starting transfers between devices  1.92 us (1%)
    all_to_all x1, blocking collectives, on_device(): lax.all_to_all(parcel, ('inp', 'tm'), split_axis=0, concat_axis=0, tiled=...  107 us
    pallas_call x1, Pallas kernels, channelize(): pl.pallas_call(channelize_kernel, grid=(half // PAIRS,), in_specs=[pl.Blo...  14.9 us
    ppermute x1, waiting for transfers between devices, passed_along(): return lax.ppermute(array, axis, pairs)  10.8 us
    pallas_call x1, Pallas kernels, correlate(): pl.pallas_call(functools.partial(correlate_kernel, frames_all), grid=(cha...  8.23 us
  transfers between devices with their start and end apart: 1, of which 1 were waited for; matrix products, arithmetic and copies ran while one was open for 0% of the time, Pallas kernels for 0%

profile of v7, /device:TPU:6, one launch (start us, length us, event | category | flops | bytes accessed | tf_op | source)
XLA Modules:
  0.0 147.4 jit_solution(6391182962362017690)
XLA Ops:
  0.0 1.5 %slice.3 = bf16[64,3,1024]{2,1,0:T(4,128)(2,1)S(1)} slice(bf16[64,64,1024]{2,1,0:T(8,128)(2,1)} %param.4), slice={[0:64], [61:64], [0:1024]} | slice | bytes 786432 | tf_op jit(solution)/shard_map/slice | solution.py:214
  1.5 0.2 copy.7
  1.7 1.9 %collective-permute-start = (bf16[64,3,1024]{2,0,1:T(8,128)(2,1)S(1)}, bf16[64,3,1024]{2,0,1:T(8,128)(2,1)S(1)}, u32[]{:S(2)}, u32[]{:S(2)}) collective-permute-start(bf16[64,3,1024]{2,0,1:T(8,128)(2,1)S(1)} %copy.7), channel_id=1, source_target_pairs={{0,1},{1,2},{2,3},{3,4},{4,5},{5,6},{6,7},{7,8},{8,9},{9,10},{10,1... | collective-permute-start | bytes 1179656 | tf_op jit(solution)/shard_map/ppermute | solution.py:27
  3.6 10.8 %collective-permute-done = bf16[64,3,1024]{2,0,1:T(8,128)(2,1)S(1)} collective-permute-done((bf16[64,3,1024]{2,0,1:T(8,128)(2,1)S(1)}, bf16[64,3,1024]{2,0,1:T(8,128)(2,1)S(1)}, u32[]{:S(2)}, u32[]{:S(2)}) %collective-permute-start) | collective-permute-done | bytes 393248 | tf_op jit(solution)/shard_map/ppermute | solution.py:27
  14.4 0.3 copy.6
  14.7 0.0 copy-start
  14.7 1.2 copy-done
  15.9 0.0 copy-start.1
  15.9 0.9 copy-done.1
  16.8 14.9 %channelize.1 = bf16[512,2,32,128]{3,2,1,0:T(8,128)(2,1)} custom-call(bf16[2,512,512]{2,1,0:T(8,128)(2,1)S(1)} %copy-done, f32[2,32,512]{2,1,0:T(8,128)S(1)} %bitcast.9, f32[4,1024]{1,0:T(4,128)} %constant.4.clone.window_ref, bf16[2,32,3,1024]{3,2,1,0:T(4,128)(2,1)S(1)} %bitcast.8, bf16[2,32,64,1024]{3,2,1,0:T(8,128)(2,1)} %bitcast.11), custom_call_target="tpu_custom_call" | custom-call | flops 4294967296 | bytes 16777216 | tf_op jit(solution)/shard_map/channelize/pallas_call | solution.py:114
  31.7 107.4 %all_to_all.5 = bf16[128,256,128]{2,1,0:T(8,128)(2,1)S(1)} all-to-all(bf16[128,256,128]{2,1,0:T(8,128)(2,1)} %bitcast.10), channel_id=1, replica_groups=mesh['inp'=8,'tm'=16] {'inp','tm'}, dimensions={0} | all-to-all | bytes 16777216 | tf_op jit(solution)/shard_map/all_to_all | solution.py:221
  139.1 8.2 %correlate.1 = f32[4,2,512,512]{3,2,1,0:T(8,128)} custom-call(bf16[8,16,4,64,128]{4,3,2,1,0:T(8,128)(2,1)S(1)} %bitcast.7), custom_call_target="tpu_custom_call" | custom-call | flops 6442450944 | bytes 16777216 | tf_op jit(solution)/shard_map/correlate/pallas_call | solution.py:187
Async XLA Ops:
  1.7 12.7 %collective-permute-start = (bf16[64,3,1024]{2,0,1:T(8,128)(2,1)S(1)}, bf16[64,3,1024]{2,0,1:T(8,128)(2,1)S(1)}, u32[]{:S(2)}, u32[]{:S(2)}) collective-permute-start(bf16[64,3,1024]{2,0,1:T(8,128)(2,1)S(1)} %copy.7), channel_id=1, source_target_pairs={{0,1},{1,2},{2,3},{3,4},{4,5},{5,6},{6,7},{7,8},{8,9},{9,10},{10,1... | collective-permute-start | bytes 1179656 | tf_op jit(solution)/shard_map/ppermute | solution.py:27
  14.7 1.2 copy-start
  15.9 0.9 copy-start.1

commit v8 on v6

--- a/solution.py
+++ b/solution.py
@@ -13,7 +13,7 @@
 TAPS = 4
 LANES = 128
 SUBLANES = 8
-BLOCK = 16
+BLOCK = 8
 EARLY_BLOCK = 32
 PAIRS = 8
 SUB = 2
@@ -64,16 +64,32 @@
             store(a, halves[1], near - far)
 
 
-def filter_late_kernel(window_ref, samples_ref, out_ref):
+def filter_late_kernel(taps_ref, samples_ref, out_ref, window_ref, held, ready, arrived):
     inputs, frames, nfft = samples_ref.shape
 
-    def rows_of(a, lanes):
-        return samples_ref[a, :, lanes].astype(jnp.float32)
-
-    def store(a, lanes, rows):
-        out_ref[a, SUBLANES:, lanes] = rows
-
-    folded(rows_of, window_ref, store, inputs, nfft)
+    def copy(k):
+        some = pl.ds(k * BLOCK, BLOCK)
+        return pltpu.make_async_copy(samples_ref.at[some], held.at[some], arrived.at[k])
+
+    taps = pltpu.make_async_copy(taps_ref, window_ref, ready)
+    taps.start()
+    for k in range(inputs // BLOCK):
+        copy(k).start()
+    taps.wait()
+
+    def step(k, carry):
+        copy(k).wait()
+
+        def rows_of(a, lanes):
+            return held[k * BLOCK + a, :, lanes].astype(jnp.float32)
+
+        def store(a, lanes, rows):
+            out_ref[k * BLOCK + a, SUBLANES:, lanes] = rows
+
+        folded(rows_of, window_ref, store, BLOCK, nfft)
+        return carry
+
+    lax.fori_loop(0, inputs // BLOCK, step, 0)
 
 
 def filter_early_kernel(window_ref, halo_ref, samples_ref, late_ref, out_ref):
@@ -95,16 +111,19 @@
     inputs, frames, nfft = samples.shape
     return pl.pallas_call(
         filter_late_kernel,
-        grid=(inputs // BLOCK,),
         in_specs=[
-            pl.BlockSpec(window.shape, lambda i: (0, 0)),
-            pl.BlockSpec((BLOCK, frames, nfft), lambda i: (i, 0, 0)),
-        ],
-        out_specs=pl.BlockSpec((BLOCK, frames, nfft), lambda i: (i, 0, 0)),
+            pl.BlockSpec(memory_space=pl.ANY),
+            pl.BlockSpec(memory_space=pl.ANY),
+        ],
+        out_specs=pl.BlockSpec(memory_space=pltpu.VMEM),
         out_shape=jax.ShapeDtypeStruct((inputs, frames, nfft), jnp.bfloat16),
-        compiler_params=pltpu.CompilerParams(
-            dimension_semantics=("arbitrary",), vmem_limit_bytes=16 * MIB
-        ),
+        scratch_shapes=[
+            pltpu.VMEM(window.shape, window.dtype),
+            pltpu.VMEM(samples.shape, samples.dtype),
+            pltpu.SemaphoreType.DMA,
+            pltpu.SemaphoreType.DMA((inputs // BLOCK,)),
+        ],
+        compiler_params=pltpu.CompilerParams(vmem_limit_bytes=16 * MIB),
         cost_estimate=pl.CostEstimate(
             flops=2 * TAPS * inputs * frames * nfft,
             transcendentals=0,

time: 142 us -> 144 us (1.014)
  transfers between devices with their start and end apart: 1 -> 1, of which waited for: 1 -> 1; matrix products, arithmetic and copies ran while one was open for 0% -> 0% of each run, Pallas kernels for 6% -> 7%
where the time goes in v8:
time: 144 us; the launch traced here: 143 us
  blocking collectives  109 us (76%)
  Pallas kernels  28.8 us (20%)
  waiting for transfers between devices  1.98 us (1%)
  starting transfers between devices  1.92 us (1%)
  local copies, waits for them, and re-layouts  1.51 us (1%)
    all_to_all x1, blocking collectives, on_device(): lax.all_to_all(parcel, ('inp', 'tm'), split_axis=0, concat_axis=0, tiled=...  109 us
    pallas_call x1, Pallas kernels, filter_late(): pl.pallas_call(filter_late_kernel, in_specs=[pl.BlockSpec(memory_space=pl...  10.2 us
    pallas_call x1, Pallas kernels, correlate(): pl.pallas_call(functools.partial(correlate_kernel, frames_all), grid=(cha...  8.23 us
    pallas_call x1, Pallas kernels, channelize(): pl.pallas_call(channelize_kernel, grid=(half // PAIRS,), in_specs=[pl.Blo...  7.74 us
  transfers between devices with their start and end apart: 1, of which 1 were waited for; matrix products, arithmetic and copies ran while one was open for 0% of the time, Pallas kernels for 7%

profile of v8, /device:TPU:6, one launch (start us, length us, event | category | flops | bytes accessed | tf_op | source)
XLA Modules:
  0.0 143.3 jit_solution(2971449084653843765)
XLA Ops:
  0.0 1.5 %slice.3 = bf16[64,3,1024]{2,1,0:T(4,128)(2,1)S(1)} slice(bf16[64,64,1024]{2,1,0:T(8,128)(2,1)} %samples_ref.3), slice={[0:64], [61:64], [0:1024]} | slice | bytes 786432 | tf_op jit(solution)/shard_map/slice | solution.py:291
  1.5 1.9 %collective-permute-start = (bf16[64,3,1024]{2,1,0:T(4,128)(2,1)S(1)}, bf16[64,3,1024]{2,1,0:T(4,128)(2,1)S(1)}, u32[]{:S(2)}, u32[]{:S(2)}) collective-permute-start(bf16[64,3,1024]{2,1,0:T(4,128)(2,1)S(1)} %slice.3), channel_id=1, source_target_pairs={{0,1},{1,2},{2,3},{3,4},{4,5},{5,6},{6,7},{7,8},{8,9},{9,10},{10,1... | collective-permute-start | bytes 1179656 | tf_op jit(solution)/shard_map/ppermute | solution.py:27
  3.4 10.2 %filter_late.1.late_ref = bf16[64,64,1024]{2,1,0:T(8,128)(2,1)S(1)} custom-call(f32[4,1024]{1,0:T(4,128)} %constant.4.clone.taps_ref.window_ref, bf16[64,64,1024]{2,1,0:T(8,128)(2,1)} %samples_ref.3), custom_call_target="tpu_custom_call" | custom-call | flops 33554432 | bytes 16777216 | tf_op jit(solution)/shard_map/filter_late/pallas_call | solution.py:112
  13.6 0.0 copy-start
  13.6 0.0 copy-start.1
  13.6 2.0 %collective-permute-done.halo_ref = bf16[64,3,1024]{2,1,0:T(4,128)(2,1)S(1)} collective-permute-done((bf16[64,3,1024]{2,1,0:T(4,128)(2,1)S(1)}, bf16[64,3,1024]{2,1,0:T(4,128)(2,1)S(1)}, u32[]{:S(2)}, u32[]{:S(2)}) %collective-permute-start) | collective-permute-done | bytes 393248 | tf_op jit(solution)/shard_map/ppermute | solution.py:27
  15.6 2.7 %filter_early.1 = bf16[64,64,1024]{2,1,0:T(8,128)(2,1)S(1)} custom-call(f32[4,1024]{1,0:T(4,128)} %constant.4.clone.taps_ref.window_ref, bf16[64,3,1024]{2,1,0:T(4,128)(2,1)S(1)} %collective-permute-done.halo_ref, bf16[64,64,1024]{2,1,0:T(8,128)(2,1)} %samples_ref.3, bf16[64,64,1024]{2,1,0:T(8,128)(2,1)S(1)} %filter_late.1.late_ref), custom_call_target="tpu_custom_call", output_to_operand_aliasing={{}: (3, {})} | custom-call | flops 4194304 | bytes 2097152 | tf_op jit(solution)/shard_map/filter_early/pallas_call | solution.py:138
  18.3 0.0 copy-done
  18.3 0.0 copy-done.1
  18.3 7.7 %channelize.1 = bf16[512,2,32,128]{3,2,1,0:T(8,128)(2,1)S(1)} custom-call(bf16[2,512,512]{2,1,0:T(8,128)(2,1)S(1)} %copy-done, f32[2,32,512]{2,1,0:T(8,128)S(1)} %bitcast.9, bf16[2,32,64,1024]{3,2,1,0:T(8,128)(2,1)S(1)} %bitcast.6), custom_call_target="tpu_custom_call" | custom-call | flops 4294967296 | bytes 16777216 | tf_op jit(solution)/shard_map/channelize/pallas_call | solution.py:201
  26.1 109.0 %all_to_all.5 = bf16[128,256,128]{2,1,0:T(8,128)(2,1)S(1)} all-to-all(bf16[128,256,128]{2,1,0:T(8,128)(2,1)S(1)} %bitcast.7), channel_id=1, replica_groups=mesh['inp'=8,'tm'=16] {'inp','tm'}, dimensions={0} | all-to-all | bytes 16777216 | tf_op jit(solution)/shard_map/all_to_all | solution.py:301
  135.1 8.2 %correlate.1 = f32[4,2,512,512]{3,2,1,0:T(8,128)} custom-call(bf16[8,16,4,64,128]{4,3,2,1,0:T(8,128)(2,1)S(1)} %bitcast.8), custom_call_target="tpu_custom_call" | custom-call | flops 6442450944 | bytes 16777216 | tf_op jit(solution)/shard_map/correlate/pallas_call | solution.py:264
Async XLA Ops:
  1.5 14.1 %collective-permute-start = (bf16[64,3,1024]{2,1,0:T(4,128)(2,1)S(1)}, bf16[64,3,1024]{2,1,0:T(4,128)(2,1)S(1)}, u32[]{:S(2)}, u32[]{:S(2)}) collective-permute-start(bf16[64,3,1024]{2,1,0:T(4,128)(2,1)S(1)} %slice.3), channel_id=1, source_target_pairs={{0,1},{1,2},{2,3},{3,4},{4,5},{5,6},{6,7},{7,8},{8,9},{9,10},{10,1... | collective-permute-start | bytes 1179656 | tf_op jit(solution)/shard_map/ppermute | solution.py:27
  13.6 4.7 %copy-start = (bf16[2,512,512]{2,1,0:T(8,128)(2,1)S(1)}, bf16[2,512,512]{2,1,0:T(8,128)(2,1)}, u32[]{:S(2)}) copy-start(bf16[2,512,512]{2,1,0:T(8,128)(2,1)} %constant.5.clone.table_ref) | copy-start | bytes 3145732
  13.6 4.7 %copy-start.1 = (f32[512,64]{0,1:T(8,128)S(1)}, f32[512,64]{0,1:T(8,128)}, u32[]{:S(2)}) copy-start(f32[512,64]{0,1:T(8,128)} %param.5) | copy-start | bytes 393220
